TPU v7x, 32 devices: a whole 2x2x4 slice. The times are simulated.
32 devices in a mesh: ctx: 8 (over z, y), dp: 4 (over x, core).
Axes of the slice: x: 2, y: 2, z: 4, core: 2. Of those that a mesh axis runs over, the one named last changes fastest.
Arguments:
- tokens: bfloat16 [4, 4096, 768], P('dp', 'ctx'), may hold values from -6 to 6
- cotangent: bfloat16 [4, 4096, 768], P('dp', 'ctx'), may hold values from -6 to 6
- attn_gain: bfloat16 [768], P('dp'), may hold values from 0.099609375 to 1.8984375
- mlp_gain: bfloat16 [768], P('dp'), may hold values from 0.099609375 to 1.8984375
- w_qkv: bfloat16 [768, 2304], P('dp'), may hold values from -0.21875 to 0.21875
- w_out: bfloat16 [768, 768], P('dp'), may hold values from -6 to 6
- w_in: bfloat16 [768, 2304], P('dp'), may hold values from -0.21875 to 0.21875
- w_mlp_out: bfloat16 [1152, 768], P('dp'), may hold values from -0.1875 to 0.1875
- block_offsets: int32 [4, 8], P('dp', 'ctx'), may hold values from 0 to 3584, as said below
Outputs:
- mixed: bfloat16 [4, 4096, 768], P('dp', 'ctx')
- tokens_grad: float32 [4, 4096, 768], P('dp', 'ctx')
- attn_gain_grad: float32 [768], P('dp')
- mlp_gain_grad: float32 [768], P('dp')
- w_qkv_grad: float32 [768, 2304], P('dp')
- w_out_grad: float32 [768, 768], P('dp')
- w_in_grad: float32 [768, 2304], P('dp')
- w_mlp_out_grad: float32 [1152, 768], P('dp')
Inputs may be any that keep to these rules, and one draw needn't show every extreme that they name: `block_offsets`: each row holds every multiple of 512 below 4096 exactly once.
All inputs are finite; a program needn't handle non-finite values.
Results may differ from a plain program's by a relative error of at most 0.022.
Values may be sent and summed in bfloat16 or wider, within the bound.
No kernel may reach another device: no remote copies, remote signals or barrier semaphores. Data moves between devices by JAX's collectives and lax.ppermute only.
A program may use at most 128 MiB of HBM per device.

v0:
```python
import jax
import jax.numpy as jnp
from jax import lax
from jax.sharding import PartitionSpec as P

HEADS = 12
HEAD_DIM = 64
FF = 1152
rope_base = 160000.0
norm_eps = 1e-05


def passed_along(x, axis, by):
    count = lax.axis_size(axis)
    return lax.ppermute(x, axis, [(i, (i + by) % count) for i in range(count)])


def layer_norm(values, gain):
    center = values - jnp.mean(values, axis=-1, keepdims=True)
    spread = jnp.mean(center * center, axis=-1, keepdims=True)
    return center * lax.rsqrt(spread + norm_eps) * gain


def norm_back(values, gain, upstream):
    _, pull = jax.vjp(layer_norm, values, gain)
    return pull(upstream)


def rotary_tables(positions, half_size):
    frequency = rope_base ** (-jnp.arange(half_size, dtype=jnp.float32) / half_size)
    angles = positions[:, None] * frequency[None, :]
    cosine = jnp.cos(angles)
    sine_table = jnp.sin(angles)
    return (jnp.concatenate([cosine, cosine], -1), jnp.concatenate([sine_table, sine_table], -1))


def rotate(values, cosine, sine_table):
    half_size = values.shape[-1] // 2
    turned = jnp.concatenate([-values[..., half_size:], values[..., :half_size]], -1)
    return values * cosine[:, None, :] + turned * sine_table[:, None, :]


def unrotate(upstream, cosine, sine_table):
    half_size = upstream.shape[-1] // 2
    turned = upstream * sine_table[:, None, :]
    return upstream * cosine[:, None, :] + jnp.concatenate(
        [turned[..., half_size:], -turned[..., :half_size]], -1
    )


def geglu(packed, hidden_size):
    return jax.nn.gelu(packed[:, :hidden_size], approximate=False) * packed[:, hidden_size:]


def product(left, right):
    return jnp.dot(left, right, preferred_element_type=jnp.float32)


def transposed_left(left, right):
    return lax.dot_general(
        left, right, (((0,), (0,)), ((), ())), preferred_element_type=jnp.float32
    )


def transposed_right(left, right):
    return lax.dot_general(
        left, right, (((1,), (1,)), ((), ())), preferred_element_type=jnp.float32
    )


def key_block():
    return 512


def body(tokens, cotangent, attn_gain, mlp_gain, w_qkv, w_out, w_in, w_mlp_out, block_offsets):
    head_count = HEADS
    head_size = HEAD_DIM
    hidden_size = FF
    model_width = head_count * head_size
    scale = head_size ** (-0.5)
    inputs = tokens[0].astype(jnp.float32)
    row_count = inputs.shape[0]
    positions = (block_offsets[0, 0] + jnp.arange(row_count, dtype=jnp.int32)).astype(jnp.float32)
    cosine, sine_table = rotary_tables(positions, head_size // 2)
    gain_one, gain_two, weight_qkv, weight_out, weight_in, weight_down = (
        lax.all_gather(attn_gain, "dp", axis=0, tiled=True),
        lax.all_gather(mlp_gain, "dp", axis=0, tiled=True),
        lax.all_gather(w_qkv, "dp", axis=0, tiled=True),
        lax.all_gather(w_out, "dp", axis=0, tiled=True),
        lax.all_gather(w_in, "dp", axis=0, tiled=True),
        lax.all_gather(w_mlp_out, "dp", axis=0, tiled=True),
    )
    first_gain = gain_one.astype(jnp.float32)
    second_gain = gain_two.astype(jnp.float32)
    normed = layer_norm(inputs, first_gain).astype(jnp.bfloat16)
    packed = product(normed, weight_qkv).reshape(row_count, 3, head_count, head_size)
    queries = rotate(packed[:, 0], cosine, sine_table).astype(jnp.bfloat16)
    keys_local = (
        rotate(packed[:, 1], cosine, sine_table)
        .astype(jnp.bfloat16)
        .reshape(row_count, model_width)
    )
    values_local = packed[:, 2].astype(jnp.bfloat16).reshape(row_count, model_width)

    def attend(carried, blocks):
        running_max, running_sum, running_out = carried
        key_part, value_part = blocks
        scores = (
            jnp.einsum("qhd,khd->hqk", queries, key_part, preferred_element_type=jnp.float32)
            * scale
        )
        new_max = jnp.maximum(running_max, jnp.max(scores, axis=-1))
        rescale = jnp.exp(running_max - new_max)
        weights = jnp.exp(scores - new_max[:, :, None])
        running_sum = running_sum * rescale + jnp.sum(weights, axis=-1)
        running_out = running_out * rescale.T[:, :, None] + jnp.einsum(
            "hqk,khd->qhd",
            weights.astype(jnp.bfloat16),
            value_part,
            preferred_element_type=jnp.float32,
        )
        return ((new_max, running_sum, running_out), None)

    initial = (
        jnp.full((head_count, row_count), -1e30, jnp.float32),
        jnp.zeros((head_count, row_count), jnp.float32),
        jnp.zeros((row_count, head_count, head_size), jnp.float32),
    )
    carried = initial
    shards = (
        lax.all_gather(keys_local, "ctx", axis=0, tiled=True),
        lax.all_gather(values_local, "ctx", axis=0, tiled=True),
    )
    key_count = shards[0].shape[0]
    block_size = key_block()
    split_keys = shards[0].reshape(key_count // block_size, block_size, head_count, head_size)
    split_values = shards[1].reshape(key_count // block_size, block_size, head_count, head_size)
    carried, _ = lax.scan(attend, carried, (split_keys, split_values))
    running_max, running_sum, running_out = carried
    attended = running_out / running_sum.T[:, :, None]
    log_total = running_max + jnp.log(running_sum)
    attended_low = attended.reshape(row_count, model_width).astype(jnp.bfloat16)
    residual = inputs + product(attended_low, weight_out)
    mlp_normed = layer_norm(residual, second_gain).astype(jnp.bfloat16)
    up_gate = product(mlp_normed, weight_in)
    joined = geglu(up_gate, hidden_size).astype(jnp.bfloat16)
    outputs = residual + product(joined, weight_down)
    mixed = outputs.astype(jnp.bfloat16)[None]
    gain_one, gain_two, weight_qkv, weight_out, weight_in, weight_down = (
        lax.all_gather(attn_gain, "dp", axis=0, tiled=True),
        lax.all_gather(mlp_gain, "dp", axis=0, tiled=True),
        lax.all_gather(w_qkv, "dp", axis=0, tiled=True),
        lax.all_gather(w_out, "dp", axis=0, tiled=True),
        lax.all_gather(w_in, "dp", axis=0, tiled=True),
        lax.all_gather(w_mlp_out, "dp", axis=0, tiled=True),
    )
    first_gain = gain_one.astype(jnp.float32)
    second_gain = gain_two.astype(jnp.float32)
    upstream = cotangent[0].astype(jnp.float32)
    upstream_low = upstream.astype(jnp.bfloat16)
    grad_down = transposed_left(joined, upstream_low)
    grad_joined = transposed_right(upstream_low, weight_down)
    _, glu_pull = jax.vjp(lambda packed_in: geglu(packed_in, hidden_size), up_gate)
    grad_up_gate = glu_pull(grad_joined)[0].astype(jnp.bfloat16)
    grad_in = transposed_left(mlp_normed, grad_up_gate)
    grad_mlp_normed = transposed_right(grad_up_gate, weight_in)
    grad_residual_norm, grad_gain_two = norm_back(residual, second_gain, grad_mlp_normed)
    grad_residual = upstream + grad_residual_norm
    residual_low = grad_residual.astype(jnp.bfloat16)
    grad_out = transposed_left(attended_low, residual_low)
    grad_attended = (
        transposed_right(residual_low, weight_out)
        .astype(jnp.bfloat16)
        .reshape(row_count, head_count, head_size)
    )
    row_delta = jnp.sum(grad_attended.astype(jnp.float32) * attended, axis=-1).T

    def block_grads(query_rows, grad_rows, log_rows, delta_rows, key_rows, value_rows):
        key_count = key_rows.shape[0]
        query_count = query_rows.shape[0]
        block_size = key_block()
        split_keys = key_rows.reshape(key_count // block_size, block_size, head_count, head_size)
        split_values = value_rows.reshape(
            key_count // block_size, block_size, head_count, head_size
        )

        def backward_block(query_grad, blocks):
            key_part, value_part = blocks
            scores = (
                jnp.einsum("qhd,khd->hqk", query_rows, key_part, preferred_element_type=jnp.float32)
                * scale
            )
            probs = jnp.exp(scores - log_rows[:, :, None])
            prob_grad = jnp.einsum(
                "qhd,khd->hqk", grad_rows, value_part, preferred_element_type=jnp.float32
            )
            score_grad = (probs * (prob_grad - delta_rows[:, :, None])).astype(jnp.bfloat16)
            value_grad = jnp.einsum(
                "hqk,qhd->khd",
                probs.astype(jnp.bfloat16),
                grad_rows,
                preferred_element_type=jnp.float32,
            )
            key_grad = (
                jnp.einsum(
                    "hqk,qhd->khd", score_grad, query_rows, preferred_element_type=jnp.float32
                )
                * scale
            )
            query_grad = (
                query_grad
                + jnp.einsum(
                    "hqk,khd->qhd", score_grad, key_part, preferred_element_type=jnp.float32
                )
                * scale
            )
            return (
                query_grad,
                (
                    key_grad.reshape(block_size, model_width),
                    value_grad.reshape(block_size, model_width),
                ),
            )

        query_start = jnp.zeros((query_count, head_count, head_size), jnp.float32)
        query_grad, (key_grad, value_grad) = lax.scan(
            backward_block, query_start, (split_keys, split_values)
        )
        return (
            query_grad,
            key_grad.reshape(key_count, model_width),
            value_grad.reshape(key_count, model_width),
        )

    zero_rows = jnp.zeros((row_count, model_width), jnp.float32)
    zero_heads = jnp.zeros((row_count, head_count, head_size), jnp.float32)

    def cycle_turn(turn_index, carried):
        key_rows, value_rows, key_sum, value_sum, query_sum = carried
        query_add, key_add, value_add = block_grads(
            queries, grad_attended, log_total, row_delta, key_rows, value_rows
        )
        key_sum = key_sum + key_add
        value_sum = value_sum + value_add
        key_rows, value_rows = passed_along((key_rows, value_rows), "ctx", 1)
        key_sum, value_sum = (
            passed_along(key_sum.astype(jnp.bfloat16), "ctx", 1).astype(key_sum.dtype),
            passed_along(value_sum.astype(jnp.bfloat16), "ctx", 1).astype(value_sum.dtype),
        )
        return (key_rows, value_rows, key_sum, value_sum, query_sum + query_add)

    start_state = (keys_local, values_local, zero_rows, zero_rows, zero_heads)
    _, _, grad_keys, grad_values, grad_queries = lax.fori_loop(
        0, lax.axis_size("ctx"), cycle_turn, start_state
    )
    query_back = unrotate(grad_queries, cosine, sine_table).reshape(row_count, model_width)
    key_back = unrotate(
        grad_keys.reshape(row_count, head_count, head_size), cosine, sine_table
    ).reshape(row_count, model_width)
    grad_packed = jnp.concatenate([query_back, key_back, grad_values], axis=1).astype(jnp.bfloat16)
    grad_qkv = transposed_left(normed, grad_packed)
    grad_normed = transposed_right(grad_packed, weight_qkv)
    grad_inputs_norm, grad_gain_one = norm_back(inputs, first_gain, grad_normed)
    tokens_grad = (grad_residual + grad_inputs_norm)[None]
    summed = (
        lax.psum_scatter(
            grad_gain_one.astype(jnp.bfloat16), "dp", scatter_dimension=0, tiled=True
        ).astype(jnp.float32),
        lax.psum_scatter(
            grad_gain_two.astype(jnp.bfloat16), "dp", scatter_dimension=0, tiled=True
        ).astype(jnp.float32),
        lax.psum_scatter(
            grad_qkv.astype(jnp.bfloat16), "dp", scatter_dimension=0, tiled=True
        ).astype(jnp.float32),
        lax.psum_scatter(
            grad_out.astype(jnp.bfloat16), "dp", scatter_dimension=0, tiled=True
        ).astype(jnp.float32),
        lax.psum_scatter(
            grad_in.astype(jnp.bfloat16), "dp", scatter_dimension=0, tiled=True
        ).astype(jnp.float32),
        lax.psum_scatter(
            grad_down.astype(jnp.bfloat16), "dp", scatter_dimension=0, tiled=True
        ).astype(jnp.float32),
    )
    totals = (
        lax.psum(summed[0].astype(jnp.bfloat16), "ctx").astype(jnp.float32),
        lax.psum(summed[1].astype(jnp.bfloat16), "ctx").astype(jnp.float32),
        lax.psum(summed[2].astype(jnp.bfloat16), "ctx").astype(jnp.float32),
        lax.psum(summed[3].astype(jnp.bfloat16), "ctx").astype(jnp.float32),
        lax.psum(summed[4].astype(jnp.bfloat16), "ctx").astype(jnp.float32),
        lax.psum(summed[5].astype(jnp.bfloat16), "ctx").astype(jnp.float32),
    )
    return (mixed, tokens_grad, totals[0], totals[1], totals[2], totals[3], totals[4], totals[5])


def solution(mesh):
    return jax.shard_map(
        body,
        mesh=mesh,
        in_specs=(
            P("dp", "ctx", None),
            P("dp", "ctx", None),
            P("dp"),
            P("dp"),
            P("dp", None),
            P("dp", None),
            P("dp", None),
            P("dp", None),
            P("dp", "ctx"),
        ),
        out_specs=(
            P("dp", "ctx", None),
            P("dp", "ctx", None),
            P("dp"),
            P("dp"),
            P("dp", None),
            P("dp", None),
            P("dp", None),
            P("dp", None),
        ),
        check_vma=False,
    )
```

profile of v0, /device:TPU:0, one launch (start us, length us, event | category | flops | bytes accessed | tf_op | source)
XLA Modules:
  0.0 1304.9 jit_solution(13983983818318694424)
XLA Ops:
  11.6 8.3 all-reduce.9
  21.6 21.4 %all-gather.7.cloned.1.call-done = bf16[768,2304]{1,0:T(8,128)(2,1)} async-done(((bf16[192,2304]{1,0:T(8,128)(2,1)}), bf16[768,2304]{1,0:T(8,128)(2,1)}) %all-gather.7.cloned.1.call-update) | async-done | bytes 3538960 | tf_op jit(solution)/shard_map/all_gather | solution.py:88
  61.9 95.1 %all-gather.9.cloned.1.call-done = bf16[4096,768]{0,1:T(8,128)(2,1)} async-done(((bf16[512,768]{0,1:T(8,128)(2,1)}), bf16[4096,768]{0,1:T(8,128)(2,1)}) %all-gather.9.cloned.1.call-update) | async-done | bytes 6291472 | tf_op jit(solution)/shard_map/all_gather | solution.py:131
  157.0 7.0 copy.35
  168.8 87.9 %all-gather.11.cloned.1.call-done = bf16[4096,768]{0,1:T(8,128)(2,1)} async-done(((bf16[512,768]{0,1:T(8,128)(2,1)}), bf16[4096,768]{0,1:T(8,128)(2,1)}) %all-gather.11.cloned.1.call-update) | async-done | bytes 6291472 | tf_op jit(solution)/shard_map/all_gather | solution.py:132
  256.7 7.0 copy.36
  268.8 145.5 %while.40 = (s32[]{:T(128)}, f32[12,512]{1,0:T(8,128)S(1)}, f32[12,512]{1,0:T(8,128)S(1)}, f32[512,12,64]{0,2,1:T(8,128)S(1)}, bf16[8,512,12,64]{1,3,2,0:T(8,128...) while((s32[]{:T(128)}, f32[12,512]{1,0:T(8,128)S(1)}, ...), condition=%wide.region_5.6_spmd.clone, body=%wide.region_2.5_spmd.clone.sunk | while | flops 831688704 | bytes 93979776 | solution.py:138
  268.8 7.4 bitcast_reduce_fusion.2
  276.3 6.4 bitcast_add_fusion.6
  288.0 7.4 bitcast_reduce_fusion.2
  295.4 6.4 bitcast_add_fusion.6
  306.1 7.4 bitcast_reduce_fusion.2
  313.5 6.7 bitcast_add_fusion.6
  324.5 7.4 bitcast_reduce_fusion.2
  342.5 7.4 bitcast_reduce_fusion.2
  360.5 7.4 bitcast_reduce_fusion.2
  378.4 7.4 bitcast_reduce_fusion.2
  396.4 7.4 bitcast_reduce_fusion.2
  419.6 6.8 fusion.82
  426.5 8.1 fusion.72
  454.6 6.4 convolution_convert_fusion
  461.1 664.6 %while.41 = (s32[]{:T(128)}, bf16[512,768]{0,1:T(8,128)(2,1)}, bf16[512,768]{0,1:T(8,128)(2,1)}, f32[512,768]{0,1:T(8,128)}, f32[512,768]{0,1:T(8,128)}, /*index...) while((s32[]{:T(128)}, bf16[512,768]{0,1:T(8,128)(2,1)}, ...), condition=%wide.region_12.13_spmd.clone, body=%wide.region_11.12_spmd.clone.sunk | while | flops 2043150336 | bytes 191177200 | solution.py:253
  475.6 6.4 fusion.152
  498.8 15.6 %collective-permute-done.3 = bf16[512,768]{0,1:T(8,128)(2,1)} collective-permute-done((bf16[512,768]{0,1:T(8,128)(2,1)}, bf16[512,768]{0,1:T(8,128)(2,1)}, u32[]{:S(2)}, u32[]{:S(2)}) %collective-permute-start.3) | collective-permute-done | bytes 786464 | tf_op jit(solution)/shard_map/while/body/eval_jaxpr/ppermute | solution.py:15
  516.9 14.3 %collective-permute-done = bf16[512,768]{0,1:T(8,128)(2,1)} collective-permute-done((bf16[512,768]{0,1:T(8,128)(2,1)S(1)}, bf16[512,768]{0,1:T(8,128)(2,1)}, u32[]{:S(2)}, u32[]{:S(2)}) %collective-permute-start) | collective-permute-done | bytes 786464 | tf_op jit(solution)/shard_map/while/body/eval_jaxpr/ppermute | solution.py:15
  531.2 14.9 %collective-permute-done.1 = bf16[512,768]{0,1:T(8,128)(2,1)} collective-permute-done((bf16[512,768]{0,1:T(8,128)(2,1)S(1)}, bf16[512,768]{0,1:T(8,128)(2,1)}, u32[]{:S(2)}, u32[]{:S(2)}) %collective-permute-start.1) | collective-permute-done | bytes 786464 | tf_op jit(solution)/shard_map/while/body/eval_jaxpr/ppermute | solution.py:15
  570.7 6.4 bitcast_add_fusion.7
  577.1 6.5 collective-permute-done.2
  585.0 15.6 %collective-permute-done.3 = bf16[512,768]{0,1:T(8,128)(2,1)} collective-permute-done((bf16[512,768]{0,1:T(8,128)(2,1)}, bf16[512,768]{0,1:T(8,128)(2,1)}, u32[]{:S(2)}, u32[]{:S(2)}) %collective-permute-start.3) | collective-permute-done | bytes 786464 | tf_op jit(solution)/shard_map/while/body/eval_jaxpr/ppermute | solution.py:15
  603.1 14.4 %collective-permute-done = bf16[512,768]{0,1:T(8,128)(2,1)} collective-permute-done((bf16[512,768]{0,1:T(8,128)(2,1)S(1)}, bf16[512,768]{0,1:T(8,128)(2,1)}, u32[]{:S(2)}, u32[]{:S(2)}) %collective-permute-start) | collective-permute-done | bytes 786464 | tf_op jit(solution)/shard_map/while/body/eval_jaxpr/ppermute | solution.py:15
  617.4 14.0 %collective-permute-done.1 = bf16[512,768]{0,1:T(8,128)(2,1)} collective-permute-done((bf16[512,768]{0,1:T(8,128)(2,1)S(1)}, bf16[512,768]{0,1:T(8,128)(2,1)}, u32[]{:S(2)}, u32[]{:S(2)}) %collective-permute-start.1) | collective-permute-done | bytes 786464 | tf_op jit(solution)/shard_map/while/body/eval_jaxpr/ppermute | solution.py:15
  654.2 6.4 bitcast_add_fusion.7
  660.6 8.4 collective-permute-done.2
  670.3 15.6 %collective-permute-done.3 = bf16[512,768]{0,1:T(8,128)(2,1)} collective-permute-done((bf16[512,768]{0,1:T(8,128)(2,1)}, bf16[512,768]{0,1:T(8,128)(2,1)}, u32[]{:S(2)}, u32[]{:S(2)}) %collective-permute-start.3) | collective-permute-done | bytes 786464 | tf_op jit(solution)/shard_map/while/body/eval_jaxpr/ppermute | solution.py:15
  688.4 14.4 %collective-permute-done = bf16[512,768]{0,1:T(8,128)(2,1)} collective-permute-done((bf16[512,768]{0,1:T(8,128)(2,1)S(1)}, bf16[512,768]{0,1:T(8,128)(2,1)}, u32[]{:S(2)}, u32[]{:S(2)}) %collective-permute-start) | collective-permute-done | bytes 786464 | tf_op jit(solution)/shard_map/while/body/eval_jaxpr/ppermute | solution.py:15
  702.8 13.1 %collective-permute-done.1 = bf16[512,768]{0,1:T(8,128)(2,1)} collective-permute-done((bf16[512,768]{0,1:T(8,128)(2,1)S(1)}, bf16[512,768]{0,1:T(8,128)(2,1)}, u32[]{:S(2)}, u32[]{:S(2)}) %collective-permute-start.1) | collective-permute-done | bytes 786464 | tf_op jit(solution)/shard_map/while/body/eval_jaxpr/ppermute | solution.py:15
  737.9 6.4 bitcast_add_fusion.7
  744.3 9.2 collective-permute-done.2
  754.9 15.6 %collective-permute-done.3 = bf16[512,768]{0,1:T(8,128)(2,1)} collective-permute-done((bf16[512,768]{0,1:T(8,128)(2,1)}, bf16[512,768]{0,1:T(8,128)(2,1)}, u32[]{:S(2)}, u32[]{:S(2)}) %collective-permute-start.3) | collective-permute-done | bytes 786464 | tf_op jit(solution)/shard_map/while/body/eval_jaxpr/ppermute | solution.py:15
  772.9 14.4 %collective-permute-done = bf16[512,768]{0,1:T(8,128)(2,1)} collective-permute-done((bf16[512,768]{0,1:T(8,128)(2,1)S(1)}, bf16[512,768]{0,1:T(8,128)(2,1)}, u32[]{:S(2)}, u32[]{:S(2)}) %collective-permute-start) | collective-permute-done | bytes 786464 | tf_op jit(solution)/shard_map/while/body/eval_jaxpr/ppermute | solution.py:15
  787.3 12.3 collective-permute-done.1
  821.4 6.4 bitcast_add_fusion.7
  827.8 9.3 collective-permute-done.2
  838.5 15.6 %collective-permute-done.3 = bf16[512,768]{0,1:T(8,128)(2,1)} collective-permute-done((bf16[512,768]{0,1:T(8,128)(2,1)}, bf16[512,768]{0,1:T(8,128)(2,1)}, u32[]{:S(2)}, u32[]{:S(2)}) %collective-permute-start.3) | collective-permute-done | bytes 786464 | tf_op jit(solution)/shard_map/while/body/eval_jaxpr/ppermute | solution.py:15
  856.6 14.4 %collective-permute-done = bf16[512,768]{0,1:T(8,128)(2,1)} collective-permute-done((bf16[512,768]{0,1:T(8,128)(2,1)S(1)}, bf16[512,768]{0,1:T(8,128)(2,1)}, u32[]{:S(2)}, u32[]{:S(2)}) %collective-permute-start) | collective-permute-done | bytes 786464 | tf_op jit(solution)/shard_map/while/body/eval_jaxpr/ppermute | solution.py:15
  871.0 11.4 collective-permute-done.1
  904.2 6.4 bitcast_add_fusion.7
  910.6 9.3 collective-permute-done.2
  921.3 15.6 %collective-permute-done.3 = bf16[512,768]{0,1:T(8,128)(2,1)} collective-permute-done((bf16[512,768]{0,1:T(8,128)(2,1)}, bf16[512,768]{0,1:T(8,128)(2,1)}, u32[]{:S(2)}, u32[]{:S(2)}) %collective-permute-start.3) | collective-permute-done | bytes 786464 | tf_op jit(solution)/shard_map/while/body/eval_jaxpr/ppermute | solution.py:15
  939.4 14.4 %collective-permute-done = bf16[512,768]{0,1:T(8,128)(2,1)} collective-permute-done((bf16[512,768]{0,1:T(8,128)(2,1)S(1)}, bf16[512,768]{0,1:T(8,128)(2,1)}, u32[]{:S(2)}, u32[]{:S(2)}) %collective-permute-start) | collective-permute-done | bytes 786464 | tf_op jit(solution)/shard_map/while/body/eval_jaxpr/ppermute | solution.py:15
  953.8 10.6 collective-permute-done.1
  986.2 6.4 bitcast_add_fusion.7
  992.6 9.3 collective-permute-done.2
  1003.2 15.6 %collective-permute-done.3 = bf16[512,768]{0,1:T(8,128)(2,1)} collective-permute-done((bf16[512,768]{0,1:T(8,128)(2,1)}, bf16[512,768]{0,1:T(8,128)(2,1)}, u32[]{:S(2)}, u32[]{:S(2)}) %collective-permute-start.3) | collective-permute-done | bytes 786464 | tf_op jit(solution)/shard_map/while/body/eval_jaxpr/ppermute | solution.py:15
  1021.3 14.4 %collective-permute-done = bf16[512,768]{0,1:T(8,128)(2,1)} collective-permute-done((bf16[512,768]{0,1:T(8,128)(2,1)S(1)}, bf16[512,768]{0,1:T(8,128)(2,1)}, u32[]{:S(2)}, u32[]{:S(2)}) %collective-permute-start) | collective-permute-done | bytes 786464 | tf_op jit(solution)/shard_map/while/body/eval_jaxpr/ppermute | solution.py:15
  1035.7 9.7 collective-permute-done.1
  1067.2 6.4 bitcast_add_fusion.7
  1073.7 9.3 collective-permute-done.2
  1084.3 15.6 %collective-permute-done.3 = bf16[512,768]{0,1:T(8,128)(2,1)} collective-permute-done((bf16[512,768]{0,1:T(8,128)(2,1)}, bf16[512,768]{0,1:T(8,128)(2,1)}, u32[]{:S(2)}, u32[]{:S(2)}) %collective-permute-start.3) | collective-permute-done | bytes 786464 | tf_op jit(solution)/shard_map/while/body/eval_jaxpr/ppermute | solution.py:15
  1102.4 14.4 %collective-permute-done = bf16[512,768]{0,1:T(8,128)(2,1)} collective-permute-done((bf16[512,768]{0,1:T(8,128)(2,1)S(1)}, bf16[512,768]{0,1:T(8,128)(2,1)}, u32[]{:S(2)}, u32[]{:S(2)}) %collective-permute-start) | collective-permute-done | bytes 786464 | tf_op jit(solution)/shard_map/while/body/eval_jaxpr/ppermute | solution.py:15
  1116.8 8.9 collective-permute-done.1
  1138.0 37.4 %reduce-scatter.5.cloned.1.call-done = bf16[192,2304]{1,0:T(8,128)(2,1)} async-done(((bf16[768,2304]{1,0:T(8,128)(2,1)}), bf16[192,2304]{1,0:T(8,128)(2,1)}) %reduce-scatter.5.cloned.1.call-update) | async-done | bytes 884752 | tf_op jit(solution)/shard_map/reduce_scatter | solution.py:272
  1188.3 22.7 %all-reduce.6 = (bf16[192]{0:T(256)(128)(2,1)S(1)}, bf16[192]{0:T(256)(128)(2,1)S(1)}) all-reduce(bf16[192]{0:T(256)(128)(2,1)S(1)} %dynamic-slice.3, bf16[192]{0:T(256)(128)(2,1)S(1)} %dynamic-slice.5), channel_id=1, replica_groups=mesh['ctx'=8,'dp'=4] {'ctx'}, use_global_device_ids=true, to_apply=%region_17.18 | all-reduce | flops 384 | bytes 1536 | tf_op jit(solution)/shard_map/psum | solution.py:286
  1217.6 74.8 %all-reduce.12.cloned.1.call-done = (bf16[192,2304]{1,0:T(8,128)(2,1)}, bf16[192,768]{1,0:T(8,128)(2,1)}, bf16[192,2304]{1,0:T(8,128)(2,1)}, bf16[288,768]{1,0:T(8,128)(2,1)}) async-done(((bf16[192,2304]{1,0:T(8,128)(2,1)}, bf16[192,768]{1,0:T(8,128)(2,1)}, bf16[192,2304]{1,0:T(8,128)(2,1)}, bf16[288,768]{1,0:T(8,128)(2,1)}), (bf16[192,2304]{1,0:T(8,128)(2,1)}, bf16[192,768]{1,0:T(8,128)(2,1)}, ...) | async-done | bytes 2506768 | tf_op jit(solution)/shard_map/psum | solution.py:288
  (465 shorter events, 378.3 us)
Async XLA Ops:
  7.2 13.9 %copy-start.14 = (bf16[1,512,768]{2,1,0:T(8,128)(2,1)S(1)}, bf16[1,512,768]{2,1,0:T(8,128)(2,1)}, u32[]{:S(2)}) copy-start(bf16[1,512,768]{2,1,0:T(8,128)(2,1)} %param.13) | copy-start | bytes 2359300
  7.2 35.9 %all-gather.7.cloned.1.call-start = ((), (), s32[]{:S(2)}) async-start(), calls=%async_computation.4 | async-start | bytes 4423680 | tf_op jit(solution)/shard_map/all_gather | solution.py:88
  7.9 149.1 %all-gather.9.cloned.1.call-start = ((), (), s32[]{:S(2)}) async-start(), calls=%async_computation.5 | async-start | bytes 7077888 | tf_op jit(solution)/shard_map/all_gather | solution.py:131
  20.0 28.8 %copy-start.38 = (f32[768]{0:T(1024)}, f32[768]{0:T(1024)S(1)}, u32[]{:S(2)}) copy-start(f32[768]{0:T(1024)S(1)} %convert_element_type.147) | copy-start | bytes 9220
  21.0 35.0 %copy-start.23 = (f32[512,64]{0,1:T(8,128)}, f32[512,64]{0,1:T(8,128)S(1)}, u32[]{:S(2)}) copy-start(f32[512,64]{0,1:T(8,128)S(1)} %pad_maximum_fusion.4) | copy-start | bytes 393220
  21.0 33.0 %copy-start.28 = (f32[512,64]{0,1:T(8,128)}, f32[512,64]{0,1:T(8,128)S(1)}, u32[]{:S(2)}) copy-start(f32[512,64]{0,1:T(8,128)S(1)} %pad_maximum_fusion.5) | copy-start | bytes 393220
  21.2 27.5 %copy-start.40 = (f32[512]{0:T(512)}, f32[512]{0:T(512)S(1)}, u32[]{:S(2)}) copy-start(f32[512]{0:T(512)S(1)} %broadcast_multiply_fusion.3) | copy-start | bytes 6148
  21.6 27.2 %copy-start.46 = (f32[512]{0:T(512)}, f32[512]{0:T(512)S(1)}, u32[]{:S(2)}) copy-start(f32[512]{0:T(512)S(1)} %fusion.44) | copy-start | bytes 6148
  21.6 27.2 %copy-start.42 = (f32[512]{0:T(512)}, f32[512]{0:T(512)S(1)}, u32[]{:S(2)}) copy-start(f32[512]{0:T(512)S(1)} %fusion.75) | copy-start | bytes 6148
  57.3 199.4 %all-gather.11.cloned.1.call-start = ((), (), s32[]{:S(2)}) async-start(), calls=%async_computation.6 | async-start | bytes 7077888 | tf_op jit(solution)/shard_map/all_gather | solution.py:132
  59.9 355.8 %all-gather.13.cloned.1.call-start = ((), (), s32[]{:S(2)}) async-start(), calls=%async_computation.7 | async-start | bytes 1474560 | tf_op jit(solution)/shard_map/all_gather | solution.py:89
  60.5 359.1 %all-gather.15.cloned.1.call-start = ((), (), s32[]{:S(2)}) async-start(), calls=%async_computation.8 | async-start | bytes 4423680 | tf_op jit(solution)/shard_map/all_gather | solution.py:90
  61.1 365.4 %all-gather.17.cloned.1.call-start = ((), (), s32[]{:S(2)}) async-start(), calls=%async_computation.9 | async-start | bytes 2211840 | tf_op jit(solution)/shard_map/all_gather | solution.py:91
  61.6 1076.3 %reduce-scatter.7.cloned.1.call-start = ((), (), s32[]{:S(2)}) async-start(), calls=%async_computation.11 | async-start | bytes 1474560 | tf_op jit(solution)/shard_map/reduce_scatter | solution.py:275
  276.2 9.6 copy-start.1
  435.8 11.0 copy-start.30
  446.7 691.2 %reduce-scatter.11.cloned.1.call-start = ((), (), s32[]{:S(2)}) async-start(), calls=%async_computation.13 | async-start | bytes 2211840 | tf_op jit(solution)/shard_map/reduce_scatter | solution.py:281
  449.1 688.9 %reduce-scatter.9.cloned.1.call-start = ((), (), s32[]{:S(2)}) async-start(), calls=%async_computation.12 | async-start | bytes 4423680 | tf_op jit(solution)/shard_map/reduce_scatter | solution.py:278
  461.0 714.4 %reduce-scatter.5.cloned.1.call-start = ((), (), s32[]{:S(2)}) async-start(), calls=%async_computation.10 | async-start | bytes 4423680 | tf_op jit(solution)/shard_map/reduce_scatter | solution.py:272
  461.1 664.6 %copy-start.29 = (f32[512,64]{0,1:T(8,128)S(1)}, f32[512,64]{0,1:T(8,128)}, u32[]{:S(2)}) copy-start(f32[512,64]{0,1:T(8,128)} %copy-done.28) | copy-start | bytes 393220
  474.1 23.3 %collective-permute-start.2 = (bf16[512,768]{0,1:T(8,128)(2,1)}, bf16[512,768]{0,1:T(8,128)(2,1)S(1)}, u32[]{:S(2)}, u32[]{:S(2)}) collective-permute-start(bf16[512,768]{0,1:T(8,128)(2,1)} %fusion.151), channel_id=1, source_target_pairs={{0,4},{4,8},{8,12},{12,16},{16,20},{20,24},{24,28},{28,0},{1,5},{5... | collective-permute-start | bytes 2359304 | tf_op jit(solution)/shard_map/while/body/eval_jaxpr/ppermute | solution.py:15
  483.4 31.0 %collective-permute-start.3 = (bf16[512,768]{0,1:T(8,128)(2,1)}, bf16[512,768]{0,1:T(8,128)(2,1)}, u32[]{:S(2)}, u32[]{:S(2)}) collective-permute-start(bf16[512,768]{0,1:T(8,128)(2,1)} %fusion.153), channel_id=1, source_target_pairs={{0,4},{4,8},{8,12},{12,16},{16,20},{20,24},{24,28},{28,0},{1,5},{5... | collective-permute-start | bytes 2359304 | tf_op jit(solution)/shard_map/while/body/eval_jaxpr/ppermute | solution.py:15
  483.4 47.8 %collective-permute-start = (bf16[512,768]{0,1:T(8,128)(2,1)S(1)}, bf16[512,768]{0,1:T(8,128)(2,1)}, u32[]{:S(2)}, u32[]{:S(2)}) collective-permute-start(bf16[512,768]{0,1:T(8,128)(2,1)S(1)} %copy.58), channel_id=1, source_target_pairs={{0,4},{4,8},{8,12},{12,16},{16,20},{20,24},{24,28},{28,0},{1,5},{5... | collective-permute-start | bytes 2359304 | tf_op jit(solution)/shard_map/while/body/eval_jaxpr/ppermute | solution.py:15
  483.4 62.7 %collective-permute-start.1 = (bf16[512,768]{0,1:T(8,128)(2,1)S(1)}, bf16[512,768]{0,1:T(8,128)(2,1)}, u32[]{:S(2)}, u32[]{:S(2)}) collective-permute-start(bf16[512,768]{0,1:T(8,128)(2,1)S(1)} %copy-done.6), channel_id=1, source_target_pairs={{0,4},{4,8},{8,12},{12,16},{16,20},{20,24},{24,28},{28,0},{1,5},{5... | collective-permute-start | bytes 2359304 | tf_op jit(solution)/shard_map/while/body/eval_jaxpr/ppermute | solution.py:15
  498.8 47.3 %copy-start.4 = (bf16[512,12,64]{0,2,1:T(8,128)(2,1)S(1)}, bf16[512,12,64]{0,2,1:T(8,128)(2,1)}, u32[]{:S(2)}) copy-start(bf16[512,12,64]{0,2,1:T(8,128)(2,1)} %copy-done.3) | copy-start | bytes 2359300 | tf_op jit(solution)/shard_map/while
  560.3 23.3 %collective-permute-start.2 = (bf16[512,768]{0,1:T(8,128)(2,1)}, bf16[512,768]{0,1:T(8,128)(2,1)S(1)}, u32[]{:S(2)}, u32[]{:S(2)}) collective-permute-start(bf16[512,768]{0,1:T(8,128)(2,1)} %fusion.151), channel_id=1, source_target_pairs={{0,4},{4,8},{8,12},{12,16},{16,20},{20,24},{24,28},{28,0},{1,5},{5... | collective-permute-start | bytes 2359304 | tf_op jit(solution)/shard_map/while/body/eval_jaxpr/ppermute | solution.py:15
  567.8 32.7 %collective-permute-start.3 = (bf16[512,768]{0,1:T(8,128)(2,1)}, bf16[512,768]{0,1:T(8,128)(2,1)}, u32[]{:S(2)}, u32[]{:S(2)}) collective-permute-start(bf16[512,768]{0,1:T(8,128)(2,1)} %fusion.153), channel_id=1, source_target_pairs={{0,4},{4,8},{8,12},{12,16},{16,20},{20,24},{24,28},{28,0},{1,5},{5... | collective-permute-start | bytes 2359304 | tf_op jit(solution)/shard_map/while/body/eval_jaxpr/ppermute | solution.py:15
  568.8 48.6 %collective-permute-start = (bf16[512,768]{0,1:T(8,128)(2,1)S(1)}, bf16[512,768]{0,1:T(8,128)(2,1)}, u32[]{:S(2)}, u32[]{:S(2)}) collective-permute-start(bf16[512,768]{0,1:T(8,128)(2,1)S(1)} %copy.58), channel_id=1, source_target_pairs={{0,4},{4,8},{8,12},{12,16},{16,20},{20,24},{24,28},{28,0},{1,5},{5... | collective-permute-start | bytes 2359304 | tf_op jit(solution)/shard_map/while/body/eval_jaxpr/ppermute | solution.py:15
  568.9 62.5 %collective-permute-start.1 = (bf16[512,768]{0,1:T(8,128)(2,1)S(1)}, bf16[512,768]{0,1:T(8,128)(2,1)}, u32[]{:S(2)}, u32[]{:S(2)}) collective-permute-start(bf16[512,768]{0,1:T(8,128)(2,1)S(1)} %copy-done.6), channel_id=1, source_target_pairs={{0,4},{4,8},{8,12},{12,16},{16,20},{20,24},{24,28},{28,0},{1,5},{5... | collective-permute-start | bytes 2359304 | tf_op jit(solution)/shard_map/while/body/eval_jaxpr/ppermute | solution.py:15
  585.0 46.5 %copy-start.4 = (bf16[512,12,64]{0,2,1:T(8,128)(2,1)S(1)}, bf16[512,12,64]{0,2,1:T(8,128)(2,1)}, u32[]{:S(2)}) copy-start(bf16[512,12,64]{0,2,1:T(8,128)(2,1)} %copy-done.3) | copy-start | bytes 2359300 | tf_op jit(solution)/shard_map/while
  645.7 23.3 %collective-permute-start.2 = (bf16[512,768]{0,1:T(8,128)(2,1)}, bf16[512,768]{0,1:T(8,128)(2,1)S(1)}, u32[]{:S(2)}, u32[]{:S(2)}) collective-permute-start(bf16[512,768]{0,1:T(8,128)(2,1)} %fusion.151), channel_id=1, source_target_pairs={{0,4},{4,8},{8,12},{12,16},{16,20},{20,24},{24,28},{28,0},{1,5},{5... | collective-permute-start | bytes 2359304 | tf_op jit(solution)/shard_map/while/body/eval_jaxpr/ppermute | solution.py:15
  653.2 32.7 %collective-permute-start.3 = (bf16[512,768]{0,1:T(8,128)(2,1)}, bf16[512,768]{0,1:T(8,128)(2,1)}, u32[]{:S(2)}, u32[]{:S(2)}) collective-permute-start(bf16[512,768]{0,1:T(8,128)(2,1)} %fusion.153), channel_id=1, source_target_pairs={{0,4},{4,8},{8,12},{12,16},{16,20},{20,24},{24,28},{28,0},{1,5},{5... | collective-permute-start | bytes 2359304 | tf_op jit(solution)/shard_map/while/body/eval_jaxpr/ppermute | solution.py:15
  653.7 49.1 %collective-permute-start = (bf16[512,768]{0,1:T(8,128)(2,1)S(1)}, bf16[512,768]{0,1:T(8,128)(2,1)}, u32[]{:S(2)}, u32[]{:S(2)}) collective-permute-start(bf16[512,768]{0,1:T(8,128)(2,1)S(1)} %copy.58), channel_id=1, source_target_pairs={{0,4},{4,8},{8,12},{12,16},{16,20},{20,24},{24,28},{28,0},{1,5},{5... | collective-permute-start | bytes 2359304 | tf_op jit(solution)/shard_map/while/body/eval_jaxpr/ppermute | solution.py:15
  653.8 62.1 %collective-permute-start.1 = (bf16[512,768]{0,1:T(8,128)(2,1)S(1)}, bf16[512,768]{0,1:T(8,128)(2,1)}, u32[]{:S(2)}, u32[]{:S(2)}) collective-permute-start(bf16[512,768]{0,1:T(8,128)(2,1)S(1)} %copy-done.6), channel_id=1, source_target_pairs={{0,4},{4,8},{8,12},{12,16},{16,20},{20,24},{24,28},{28,0},{1,5},{5... | collective-permute-start | bytes 2359304 | tf_op jit(solution)/shard_map/while/body/eval_jaxpr/ppermute | solution.py:15
  670.3 45.6 %copy-start.4 = (bf16[512,12,64]{0,2,1:T(8,128)(2,1)S(1)}, bf16[512,12,64]{0,2,1:T(8,128)(2,1)}, u32[]{:S(2)}) copy-start(bf16[512,12,64]{0,2,1:T(8,128)(2,1)} %copy-done.3) | copy-start | bytes 2359300 | tf_op jit(solution)/shard_map/while
  730.2 23.3 %collective-permute-start.2 = (bf16[512,768]{0,1:T(8,128)(2,1)}, bf16[512,768]{0,1:T(8,128)(2,1)S(1)}, u32[]{:S(2)}, u32[]{:S(2)}) collective-permute-start(bf16[512,768]{0,1:T(8,128)(2,1)} %fusion.151), channel_id=1, source_target_pairs={{0,4},{4,8},{8,12},{12,16},{16,20},{20,24},{24,28},{28,0},{1,5},{5... | collective-permute-start | bytes 2359304 | tf_op jit(solution)/shard_map/while/body/eval_jaxpr/ppermute | solution.py:15
  737.7 32.7 %collective-permute-start.3 = (bf16[512,768]{0,1:T(8,128)(2,1)}, bf16[512,768]{0,1:T(8,128)(2,1)}, u32[]{:S(2)}, u32[]{:S(2)}) collective-permute-start(bf16[512,768]{0,1:T(8,128)(2,1)} %fusion.153), channel_id=1, source_target_pairs={{0,4},{4,8},{8,12},{12,16},{16,20},{20,24},{24,28},{28,0},{1,5},{5... | collective-permute-start | bytes 2359304 | tf_op jit(solution)/shard_map/while/body/eval_jaxpr/ppermute | solution.py:15
  737.8 49.5 %collective-permute-start = (bf16[512,768]{0,1:T(8,128)(2,1)S(1)}, bf16[512,768]{0,1:T(8,128)(2,1)}, u32[]{:S(2)}, u32[]{:S(2)}) collective-permute-start(bf16[512,768]{0,1:T(8,128)(2,1)S(1)} %copy.58), channel_id=1, source_target_pairs={{0,4},{4,8},{8,12},{12,16},{16,20},{20,24},{24,28},{28,0},{1,5},{5... | collective-permute-start | bytes 2359304 | tf_op jit(solution)/shard_map/while/body/eval_jaxpr/ppermute | solution.py:15
  737.9 61.7 %collective-permute-start.1 = (bf16[512,768]{0,1:T(8,128)(2,1)S(1)}, bf16[512,768]{0,1:T(8,128)(2,1)}, u32[]{:S(2)}, u32[]{:S(2)}) collective-permute-start(bf16[512,768]{0,1:T(8,128)(2,1)S(1)} %copy-done.6), channel_id=1, source_target_pairs={{0,4},{4,8},{8,12},{12,16},{16,20},{20,24},{24,28},{28,0},{1,5},{5... | collective-permute-start | bytes 2359304 | tf_op jit(solution)/shard_map/while/body/eval_jaxpr/ppermute | solution.py:15
  754.8 44.7 %copy-start.4 = (bf16[512,12,64]{0,2,1:T(8,128)(2,1)S(1)}, bf16[512,12,64]{0,2,1:T(8,128)(2,1)}, u32[]{:S(2)}) copy-start(bf16[512,12,64]{0,2,1:T(8,128)(2,1)} %copy-done.3) | copy-start | bytes 2359300 | tf_op jit(solution)/shard_map/while
  813.8 23.3 %collective-permute-start.2 = (bf16[512,768]{0,1:T(8,128)(2,1)}, bf16[512,768]{0,1:T(8,128)(2,1)S(1)}, u32[]{:S(2)}, u32[]{:S(2)}) collective-permute-start(bf16[512,768]{0,1:T(8,128)(2,1)} %fusion.151), channel_id=1, source_target_pairs={{0,4},{4,8},{8,12},{12,16},{16,20},{20,24},{24,28},{28,0},{1,5},{5... | collective-permute-start | bytes 2359304 | tf_op jit(solution)/shard_map/while/body/eval_jaxpr/ppermute | solution.py:15
  821.4 32.7 %collective-permute-start.3 = (bf16[512,768]{0,1:T(8,128)(2,1)}, bf16[512,768]{0,1:T(8,128)(2,1)}, u32[]{:S(2)}, u32[]{:S(2)}) collective-permute-start(bf16[512,768]{0,1:T(8,128)(2,1)} %fusion.153), channel_id=1, source_target_pairs={{0,4},{4,8},{8,12},{12,16},{16,20},{20,24},{24,28},{28,0},{1,5},{5... | collective-permute-start | bytes 2359304 | tf_op jit(solution)/shard_map/while/body/eval_jaxpr/ppermute | solution.py:15
  821.4 49.6 %collective-permute-start = (bf16[512,768]{0,1:T(8,128)(2,1)S(1)}, bf16[512,768]{0,1:T(8,128)(2,1)}, u32[]{:S(2)}, u32[]{:S(2)}) collective-permute-start(bf16[512,768]{0,1:T(8,128)(2,1)S(1)} %copy.58), channel_id=1, source_target_pairs={{0,4},{4,8},{8,12},{12,16},{16,20},{20,24},{24,28},{28,0},{1,5},{5... | collective-permute-start | bytes 2359304 | tf_op jit(solution)/shard_map/while/body/eval_jaxpr/ppermute | solution.py:15
  821.4 61.0 %collective-permute-start.1 = (bf16[512,768]{0,1:T(8,128)(2,1)S(1)}, bf16[512,768]{0,1:T(8,128)(2,1)}, u32[]{:S(2)}, u32[]{:S(2)}) collective-permute-start(bf16[512,768]{0,1:T(8,128)(2,1)S(1)} %copy-done.6), channel_id=1, source_target_pairs={{0,4},{4,8},{8,12},{12,16},{16,20},{20,24},{24,28},{28,0},{1,5},{5... | collective-permute-start | bytes 2359304 | tf_op jit(solution)/shard_map/while/body/eval_jaxpr/ppermute | solution.py:15
  838.5 43.9 %copy-start.4 = (bf16[512,12,64]{0,2,1:T(8,128)(2,1)S(1)}, bf16[512,12,64]{0,2,1:T(8,128)(2,1)}, u32[]{:S(2)}) copy-start(bf16[512,12,64]{0,2,1:T(8,128)(2,1)} %copy-done.3) | copy-start | bytes 2359300 | tf_op jit(solution)/shard_map/while
  896.6 23.3 %collective-permute-start.2 = (bf16[512,768]{0,1:T(8,128)(2,1)}, bf16[512,768]{0,1:T(8,128)(2,1)S(1)}, u32[]{:S(2)}, u32[]{:S(2)}) collective-permute-start(bf16[512,768]{0,1:T(8,128)(2,1)} %fusion.151), channel_id=1, source_target_pairs={{0,4},{4,8},{8,12},{12,16},{16,20},{20,24},{24,28},{28,0},{1,5},{5... | collective-permute-start | bytes 2359304 | tf_op jit(solution)/shard_map/while/body/eval_jaxpr/ppermute | solution.py:15
  904.2 32.7 %collective-permute-start.3 = (bf16[512,768]{0,1:T(8,128)(2,1)}, bf16[512,768]{0,1:T(8,128)(2,1)}, u32[]{:S(2)}, u32[]{:S(2)}) collective-permute-start(bf16[512,768]{0,1:T(8,128)(2,1)} %fusion.153), channel_id=1, source_target_pairs={{0,4},{4,8},{8,12},{12,16},{16,20},{20,24},{24,28},{28,0},{1,5},{5... | collective-permute-start | bytes 2359304 | tf_op jit(solution)/shard_map/while/body/eval_jaxpr/ppermute | solution.py:15
  904.2 49.6 %collective-permute-start = (bf16[512,768]{0,1:T(8,128)(2,1)S(1)}, bf16[512,768]{0,1:T(8,128)(2,1)}, u32[]{:S(2)}, u32[]{:S(2)}) collective-permute-start(bf16[512,768]{0,1:T(8,128)(2,1)S(1)} %copy.58), channel_id=1, source_target_pairs={{0,4},{4,8},{8,12},{12,16},{16,20},{20,24},{24,28},{28,0},{1,5},{5... | collective-permute-start | bytes 2359304 | tf_op jit(solution)/shard_map/while/body/eval_jaxpr/ppermute | solution.py:15
  904.2 60.2 %collective-permute-start.1 = (bf16[512,768]{0,1:T(8,128)(2,1)S(1)}, bf16[512,768]{0,1:T(8,128)(2,1)}, u32[]{:S(2)}, u32[]{:S(2)}) collective-permute-start(bf16[512,768]{0,1:T(8,128)(2,1)S(1)} %copy-done.6), channel_id=1, source_target_pairs={{0,4},{4,8},{8,12},{12,16},{16,20},{20,24},{24,28},{28,0},{1,5},{5... | collective-permute-start | bytes 2359304 | tf_op jit(solution)/shard_map/while/body/eval_jaxpr/ppermute | solution.py:15
  921.3 43.0 %copy-start.4 = (bf16[512,12,64]{0,2,1:T(8,128)(2,1)S(1)}, bf16[512,12,64]{0,2,1:T(8,128)(2,1)}, u32[]{:S(2)}) copy-start(bf16[512,12,64]{0,2,1:T(8,128)(2,1)} %copy-done.3) | copy-start | bytes 2359300 | tf_op jit(solution)/shard_map/while
  978.6 23.3 %collective-permute-start.2 = (bf16[512,768]{0,1:T(8,128)(2,1)}, bf16[512,768]{0,1:T(8,128)(2,1)S(1)}, u32[]{:S(2)}, u32[]{:S(2)}) collective-permute-start(bf16[512,768]{0,1:T(8,128)(2,1)} %fusion.151), channel_id=1, source_target_pairs={{0,4},{4,8},{8,12},{12,16},{16,20},{20,24},{24,28},{28,0},{1,5},{5... | collective-permute-start | bytes 2359304 | tf_op jit(solution)/shard_map/while/body/eval_jaxpr/ppermute | solution.py:15
  986.1 32.7 %collective-permute-start.3 = (bf16[512,768]{0,1:T(8,128)(2,1)}, bf16[512,768]{0,1:T(8,128)(2,1)}, u32[]{:S(2)}, u32[]{:S(2)}) collective-permute-start(bf16[512,768]{0,1:T(8,128)(2,1)} %fusion.153), channel_id=1, source_target_pairs={{0,4},{4,8},{8,12},{12,16},{16,20},{20,24},{24,28},{28,0},{1,5},{5... | collective-permute-start | bytes 2359304 | tf_op jit(solution)/shard_map/while/body/eval_jaxpr/ppermute | solution.py:15
  986.1 49.6 %collective-permute-start = (bf16[512,768]{0,1:T(8,128)(2,1)S(1)}, bf16[512,768]{0,1:T(8,128)(2,1)}, u32[]{:S(2)}, u32[]{:S(2)}) collective-permute-start(bf16[512,768]{0,1:T(8,128)(2,1)S(1)} %copy.58), channel_id=1, source_target_pairs={{0,4},{4,8},{8,12},{12,16},{16,20},{20,24},{24,28},{28,0},{1,5},{5... | collective-permute-start | bytes 2359304 | tf_op jit(solution)/shard_map/while/body/eval_jaxpr/ppermute | solution.py:15
  986.1 59.3 %collective-permute-start.1 = (bf16[512,768]{0,1:T(8,128)(2,1)S(1)}, bf16[512,768]{0,1:T(8,128)(2,1)}, u32[]{:S(2)}, u32[]{:S(2)}) collective-permute-start(bf16[512,768]{0,1:T(8,128)(2,1)S(1)} %copy-done.6), channel_id=1, source_target_pairs={{0,4},{4,8},{8,12},{12,16},{16,20},{20,24},{24,28},{28,0},{1,5},{5... | collective-permute-start | bytes 2359304 | tf_op jit(solution)/shard_map/while/body/eval_jaxpr/ppermute | solution.py:15
  1003.2 42.2 %copy-start.4 = (bf16[512,12,64]{0,2,1:T(8,128)(2,1)S(1)}, bf16[512,12,64]{0,2,1:T(8,128)(2,1)}, u32[]{:S(2)}) copy-start(bf16[512,12,64]{0,2,1:T(8,128)(2,1)} %copy-done.3) | copy-start | bytes 2359300 | tf_op jit(solution)/shard_map/while
  1059.6 23.3 %collective-permute-start.2 = (bf16[512,768]{0,1:T(8,128)(2,1)}, bf16[512,768]{0,1:T(8,128)(2,1)S(1)}, u32[]{:S(2)}, u32[]{:S(2)}) collective-permute-start(bf16[512,768]{0,1:T(8,128)(2,1)} %fusion.151), channel_id=1, source_target_pairs={{0,4},{4,8},{8,12},{12,16},{16,20},{20,24},{24,28},{28,0},{1,5},{5... | collective-permute-start | bytes 2359304 | tf_op jit(solution)/shard_map/while/body/eval_jaxpr/ppermute | solution.py:15
  1067.2 32.7 %collective-permute-start.3 = (bf16[512,768]{0,1:T(8,128)(2,1)}, bf16[512,768]{0,1:T(8,128)(2,1)}, u32[]{:S(2)}, u32[]{:S(2)}) collective-permute-start(bf16[512,768]{0,1:T(8,128)(2,1)} %fusion.153), channel_id=1, source_target_pairs={{0,4},{4,8},{8,12},{12,16},{16,20},{20,24},{24,28},{28,0},{1,5},{5... | collective-permute-start | bytes 2359304 | tf_op jit(solution)/shard_map/while/body/eval_jaxpr/ppermute | solution.py:15
  1067.2 49.6 %collective-permute-start = (bf16[512,768]{0,1:T(8,128)(2,1)S(1)}, bf16[512,768]{0,1:T(8,128)(2,1)}, u32[]{:S(2)}, u32[]{:S(2)}) collective-permute-start(bf16[512,768]{0,1:T(8,128)(2,1)S(1)} %copy.58), channel_id=1, source_target_pairs={{0,4},{4,8},{8,12},{12,16},{16,20},{20,24},{24,28},{28,0},{1,5},{5... | collective-permute-start | bytes 2359304 | tf_op jit(solution)/shard_map/while/body/eval_jaxpr/ppermute | solution.py:15
  1067.2 58.4 %collective-permute-start.1 = (bf16[512,768]{0,1:T(8,128)(2,1)S(1)}, bf16[512,768]{0,1:T(8,128)(2,1)}, u32[]{:S(2)}, u32[]{:S(2)}) collective-permute-start(bf16[512,768]{0,1:T(8,128)(2,1)S(1)} %copy-done.6), channel_id=1, source_target_pairs={{0,4},{4,8},{8,12},{12,16},{16,20},{20,24},{24,28},{28,0},{1,5},{5... | collective-permute-start | bytes 2359304 | tf_op jit(solution)/shard_map/while/body/eval_jaxpr/ppermute | solution.py:15
  1084.3 41.3 %copy-start.4 = (bf16[512,12,64]{0,2,1:T(8,128)(2,1)S(1)}, bf16[512,12,64]{0,2,1:T(8,128)(2,1)}, u32[]{:S(2)}) copy-start(bf16[512,12,64]{0,2,1:T(8,128)(2,1)} %copy-done.3) | copy-start | bytes 2359300 | tf_op jit(solution)/shard_map/while
  1137.6 154.8 %all-reduce.12.cloned.1.call-start = ((), (), s32[]{:S(2)}) async-start(), calls=%async_computation.14 | async-start | bytes 5013504 | tf_op jit(solution)/shard_map/psum | solution.py:288
  1180.4 31.7 %copy-start.13 = (f32[512,768]{1,0:T(8,128)S(1)}, f32[512,768]{1,0:T(8,128)}, u32[]{:S(2)}) copy-start(f32[512,768]{1,0:T(8,128)} %copy-done.12) | copy-start | bytes 4718596
  1180.4 31.7 %copy-start.26 = (bf16[1,512,768]{2,1,0:T(8,128)(2,1)S(1)}, bf16[1,512,768]{2,1,0:T(8,128)(2,1)}, u32[]{:S(2)}) copy-start(bf16[1,512,768]{2,1,0:T(8,128)(2,1)} %param.14) | copy-start | bytes 2359300
  1180.4 31.7 %copy-start.45 = (f32[512]{0:T(512)S(1)}, f32[512]{0:T(512)}, u32[]{:S(2)}) copy-start(f32[512]{0:T(512)} %copy-done.44) | copy-start | bytes 6148
  (87 other events, 310.4 us)
Sparse Core Ops, SparseCore 0:
  9.5 33.4 all-gather.6
  57.5 99.4 all-gather.8
  159.0 97.6 all-gather.10
  258.1 15.6 all-gather.12
  275.2 30.7 all-gather.14
  307.4 20.7 all-gather.16
  446.8 23.7 reduce-scatter.6
  473.8 29.1 reduce-scatter.10
  505.6 40.3 reduce-scatter.8
  1137.8 37.5 reduce-scatter.4
  1179.3 113.0 all-reduce.11
where the time goes:
time: 1310 us; the launch traced here: 1300 us
  waiting for transfers between devices  720 us (55%)
  matrix products  312 us (24%)
  local copies, waits for them, and re-layouts  107 us (8%)
  other arithmetic  102 us (8%)
  blocking collectives  36.8 us (3%)
  between operations  16.7 us (1%)
    ppermute x32, waiting for transfers between devices, passed_along(): return lax.ppermute(x, axis, [(i, (i + by) % count) for i in range(count)])  401 us
    all_gather x1, waiting for transfers between devices, body(): lax.all_gather(keys_local, 'ctx', axis=0, tiled=True)  95.1 us
    all_gather x1, waiting for transfers between devices, body(): lax.all_gather(values_local, 'ctx', axis=0, tiled=True)  87.9 us
    psum x1, waiting for transfers between devices, body(): lax.psum(summed[2].astype(jnp.bfloat16), 'ctx').astype(jnp.float32)  74.8 us
    dot_general x8, matrix products, attend(): jnp.einsum('qhd,khd->hqk', queries, key_part, preferred_element_type=jnp....  59.3 us
    while x152, local copies, waits for them, and re-layouts  56.3 us
    dot_general x8, matrix products, attend(): jnp.einsum('hqk,khd->qhd', weights.astype(jnp.bfloat16), value_part, pref...  50.9 us
    dot_general x8, matrix products, backward_block(): jnp.einsum('hqk,khd->qhd', score_grad, key_part, preferred_element_type=j...  50.8 us
  transfers between devices with their start and end apart: 43, of which 37 were waited for; matrix products, arithmetic and copies ran while one was open for 33% of the time, Pallas kernels for 0%

commit v1 on v0

--- a/solution.py
+++ b/solution.py
@@ -8,6 +8,7 @@
 FF = 1152
 rope_base = 160000.0
 norm_eps = 1e-05
+cut_indices = lambda my_data: jnp.sum(lax.all_gather(my_data, axis_name="ctx"), axis=0)
 
 
 def passed_along(x, axis, by):
@@ -285,7 +286,7 @@
     totals = (
         lax.psum(summed[0].astype(jnp.bfloat16), "ctx").astype(jnp.float32),
         lax.psum(summed[1].astype(jnp.bfloat16), "ctx").astype(jnp.float32),
-        lax.psum(summed[2].astype(jnp.bfloat16), "ctx").astype(jnp.float32),
+        cut_indices(summed[2].astype(jnp.bfloat16)).astype(jnp.float32),
         lax.psum(summed[3].astype(jnp.bfloat16), "ctx").astype(jnp.float32),
         lax.psum(summed[4].astype(jnp.bfloat16), "ctx").astype(jnp.float32),
         lax.psum(summed[5].astype(jnp.bfloat16), "ctx").astype(jnp.float32),

time: 1310 us -> 1400 us (1.069)
  waiting for transfers between devices: 720 us -> 804 us
    all_gather x0 -> x1, waiting for transfers between devices: none -> 105 us  [lax.all_gather(my_data, axis_name='ctx')]
    psum x1, waiting for transfers between devices: 74.8 us -> 53.4 us  [body(): lax.psum(summed[3].astype(jnp.bfloat16), 'ctx').astype(jnp.float32)]
    unnamed x99 -> x97, local copies, waits for them, and re-layouts: 41.2 us -> 41.3 us
  transfers between devices with their start and end apart: 43 -> 44, of which waited for: 37 -> 38; matrix products, arithmetic and copies ran while one was open for 33% -> 32% of each run, Pallas kernels for 0% -> 0%
where the time goes in v1:
time: 1400 us; the launch traced here: 1390 us
  waiting for transfers between devices  804 us (57%)
  matrix products  312 us (22%)
  local copies, waits for them, and re-layouts  107 us (8%)
  other arithmetic  106 us (8%)
  blocking collectives  36.1 us (3%)
  between operations  17.1 us (1%)
    ppermute x32, waiting for transfers between devices, passed_along(): return lax.ppermute(x, axis, [(i, (i + by) % count) for i in range(count)])  401 us
    all_gather x1, waiting for transfers between devices, lax.all_gather(my_data, axis_name='ctx')  105 us
    all_gather x1, waiting for transfers between devices, body(): lax.all_gather(keys_local, 'ctx', axis=0, tiled=True)  95.1 us
    all_gather x1, waiting for transfers between devices, body(): lax.all_gather(values_local, 'ctx', axis=0, tiled=True)  87.9 us
    dot_general x8, matrix products, attend(): jnp.einsum('qhd,khd->hqk', queries, key_part, preferred_element_type=jnp....  59.4 us
    while x152, local copies, waits for them, and re-layouts  56.4 us
    psum x1, waiting for transfers between devices, body(): lax.psum(summed[3].astype(jnp.bfloat16), 'ctx').astype(jnp.float32)  53.4 us
    dot_general x8, matrix products, attend(): jnp.einsum('hqk,khd->qhd', weights.astype(jnp.bfloat16), value_part, pref...  50.9 us
  transfers between devices with their start and end apart: 44, of which 38 were waited for; matrix products, arithmetic and copies ran while one was open for 32% of the time, Pallas kernels for 0%

profile of v1, /device:TPU:0, one launch (start us, length us, event | category | flops | bytes accessed | tf_op | source)
XLA Modules:
  0.0 1392.8 jit_solution(6642262048987455683)
XLA Ops:
  11.6 8.3 all-reduce.9
  21.6 21.4 %all-gather.9.cloned.1.call-done = bf16[768,2304]{1,0:T(8,128)(2,1)} async-done(((bf16[192,2304]{1,0:T(8,128)(2,1)}), bf16[768,2304]{1,0:T(8,128)(2,1)}) %all-gather.9.cloned.1.call-update) | async-done | bytes 3538960 | tf_op jit(solution)/shard_map/all_gather | solution.py:89
  61.8 95.1 %all-gather.11.cloned.1.call-done = bf16[4096,768]{0,1:T(8,128)(2,1)} async-done(((bf16[512,768]{0,1:T(8,128)(2,1)}), bf16[4096,768]{0,1:T(8,128)(2,1)}) %all-gather.11.cloned.1.call-update) | async-done | bytes 6291472 | tf_op jit(solution)/shard_map/all_gather | solution.py:132
  156.9 7.0 copy.35
  168.8 87.9 %all-gather.13.cloned.1.call-done = bf16[4096,768]{0,1:T(8,128)(2,1)} async-done(((bf16[512,768]{0,1:T(8,128)(2,1)}), bf16[4096,768]{0,1:T(8,128)(2,1)}) %all-gather.13.cloned.1.call-update) | async-done | bytes 6291472 | tf_op jit(solution)/shard_map/all_gather | solution.py:133
  256.6 7.0 copy.36
  268.7 145.6 %while.40 = (s32[]{:T(128)}, f32[12,512]{1,0:T(8,128)S(1)}, f32[12,512]{1,0:T(8,128)S(1)}, f32[512,12,64]{0,2,1:T(8,128)S(1)}, bf16[8,512,12,64]{1,3,2,0:T(8,128...) while((s32[]{:T(128)}, f32[12,512]{1,0:T(8,128)S(1)}, ...), condition=%wide.region_5.6_spmd.clone, body=%wide.region_2.5_spmd.clone.sunk | while | flops 831688704 | bytes 93979776 | solution.py:139
  268.7 7.4 bitcast_reduce_fusion.2
  287.9 7.4 bitcast_reduce_fusion.2
  295.3 6.4 bitcast_add_fusion.6
  306.0 7.4 bitcast_reduce_fusion.2
  313.4 6.7 bitcast_add_fusion.6
  324.4 7.4 bitcast_reduce_fusion.2
  342.4 7.4 bitcast_reduce_fusion.2
  360.4 7.4 bitcast_reduce_fusion.2
  378.4 7.4 bitcast_reduce_fusion.2
  396.3 7.4 bitcast_reduce_fusion.2
  419.5 6.8 fusion.82
  426.4 8.1 fusion.72
  454.5 6.4 convolution_convert_fusion
  461.0 664.6 %while.41 = (s32[]{:T(128)}, bf16[512,768]{0,1:T(8,128)(2,1)}, bf16[512,768]{0,1:T(8,128)(2,1)}, f32[512,768]{0,1:T(8,128)}, f32[512,768]{0,1:T(8,128)}, /*index...) while((s32[]{:T(128)}, bf16[512,768]{0,1:T(8,128)(2,1)}, ...), condition=%wide.region_12.13_spmd.clone, body=%wide.region_11.12_spmd.clone.sunk | while | flops 2043150336 | bytes 191177200 | solution.py:254
  475.6 6.4 fusion.152
  498.7 15.6 %collective-permute-done.3 = bf16[512,768]{0,1:T(8,128)(2,1)} collective-permute-done((bf16[512,768]{0,1:T(8,128)(2,1)}, bf16[512,768]{0,1:T(8,128)(2,1)}, u32[]{:S(2)}, u32[]{:S(2)}) %collective-permute-start.3) | collective-permute-done | bytes 786464 | tf_op jit(solution)/shard_map/while/body/eval_jaxpr/ppermute | solution.py:16
  516.8 14.3 %collective-permute-done = bf16[512,768]{0,1:T(8,128)(2,1)} collective-permute-done((bf16[512,768]{0,1:T(8,128)(2,1)S(1)}, bf16[512,768]{0,1:T(8,128)(2,1)}, u32[]{:S(2)}, u32[]{:S(2)}) %collective-permute-start) | collective-permute-done | bytes 786464 | tf_op jit(solution)/shard_map/while/body/eval_jaxpr/ppermute | solution.py:16
  531.1 14.8 %collective-permute-done.1 = bf16[512,768]{0,1:T(8,128)(2,1)} collective-permute-done((bf16[512,768]{0,1:T(8,128)(2,1)S(1)}, bf16[512,768]{0,1:T(8,128)(2,1)}, u32[]{:S(2)}, u32[]{:S(2)}) %collective-permute-start.1) | collective-permute-done | bytes 786464 | tf_op jit(solution)/shard_map/while/body/eval_jaxpr/ppermute | solution.py:16
  570.7 6.4 bitcast_add_fusion.7
  577.1 6.5 collective-permute-done.2
  584.9 15.6 %collective-permute-done.3 = bf16[512,768]{0,1:T(8,128)(2,1)} collective-permute-done((bf16[512,768]{0,1:T(8,128)(2,1)}, bf16[512,768]{0,1:T(8,128)(2,1)}, u32[]{:S(2)}, u32[]{:S(2)}) %collective-permute-start.3) | collective-permute-done | bytes 786464 | tf_op jit(solution)/shard_map/while/body/eval_jaxpr/ppermute | solution.py:16
  603.0 14.4 %collective-permute-done = bf16[512,768]{0,1:T(8,128)(2,1)} collective-permute-done((bf16[512,768]{0,1:T(8,128)(2,1)S(1)}, bf16[512,768]{0,1:T(8,128)(2,1)}, u32[]{:S(2)}, u32[]{:S(2)}) %collective-permute-start) | collective-permute-done | bytes 786464 | tf_op jit(solution)/shard_map/while/body/eval_jaxpr/ppermute | solution.py:16
  617.4 14.0 %collective-permute-done.1 = bf16[512,768]{0,1:T(8,128)(2,1)} collective-permute-done((bf16[512,768]{0,1:T(8,128)(2,1)S(1)}, bf16[512,768]{0,1:T(8,128)(2,1)}, u32[]{:S(2)}, u32[]{:S(2)}) %collective-permute-start.1) | collective-permute-done | bytes 786464 | tf_op jit(solution)/shard_map/while/body/eval_jaxpr/ppermute | solution.py:16
  654.1 6.4 bitcast_add_fusion.7
  660.5 8.4 collective-permute-done.2
  670.3 15.6 %collective-permute-done.3 = bf16[512,768]{0,1:T(8,128)(2,1)} collective-permute-done((bf16[512,768]{0,1:T(8,128)(2,1)}, bf16[512,768]{0,1:T(8,128)(2,1)}, u32[]{:S(2)}, u32[]{:S(2)}) %collective-permute-start.3) | collective-permute-done | bytes 786464 | tf_op jit(solution)/shard_map/while/body/eval_jaxpr/ppermute | solution.py:16
  688.4 14.4 %collective-permute-done = bf16[512,768]{0,1:T(8,128)(2,1)} collective-permute-done((bf16[512,768]{0,1:T(8,128)(2,1)S(1)}, bf16[512,768]{0,1:T(8,128)(2,1)}, u32[]{:S(2)}, u32[]{:S(2)}) %collective-permute-start) | collective-permute-done | bytes 786464 | tf_op jit(solution)/shard_map/while/body/eval_jaxpr/ppermute | solution.py:16
  702.7 13.1 collective-permute-done.1
  737.9 6.4 bitcast_add_fusion.7
  744.2 9.2 collective-permute-done.2
  754.8 15.6 %collective-permute-done.3 = bf16[512,768]{0,1:T(8,128)(2,1)} collective-permute-done((bf16[512,768]{0,1:T(8,128)(2,1)}, bf16[512,768]{0,1:T(8,128)(2,1)}, u32[]{:S(2)}, u32[]{:S(2)}) %collective-permute-start.3) | collective-permute-done | bytes 786464 | tf_op jit(solution)/shard_map/while/body/eval_jaxpr/ppermute | solution.py:16
  772.9 14.4 %collective-permute-done = bf16[512,768]{0,1:T(8,128)(2,1)} collective-permute-done((bf16[512,768]{0,1:T(8,128)(2,1)S(1)}, bf16[512,768]{0,1:T(8,128)(2,1)}, u32[]{:S(2)}, u32[]{:S(2)}) %collective-permute-start) | collective-permute-done | bytes 786464 | tf_op jit(solution)/shard_map/while/body/eval_jaxpr/ppermute | solution.py:16
  787.2 12.3 collective-permute-done.1
  821.4 6.4 bitcast_add_fusion.7
  827.8 9.3 collective-permute-done.2
  838.4 15.6 %collective-permute-done.3 = bf16[512,768]{0,1:T(8,128)(2,1)} collective-permute-done((bf16[512,768]{0,1:T(8,128)(2,1)}, bf16[512,768]{0,1:T(8,128)(2,1)}, u32[]{:S(2)}, u32[]{:S(2)}) %collective-permute-start.3) | collective-permute-done | bytes 786464 | tf_op jit(solution)/shard_map/while/body/eval_jaxpr/ppermute | solution.py:16
  856.5 14.4 %collective-permute-done = bf16[512,768]{0,1:T(8,128)(2,1)} collective-permute-done((bf16[512,768]{0,1:T(8,128)(2,1)S(1)}, bf16[512,768]{0,1:T(8,128)(2,1)}, u32[]{:S(2)}, u32[]{:S(2)}) %collective-permute-start) | collective-permute-done | bytes 786464 | tf_op jit(solution)/shard_map/while/body/eval_jaxpr/ppermute | solution.py:16
  870.9 11.4 collective-permute-done.1
  904.2 6.4 bitcast_add_fusion.7
  910.6 9.3 collective-permute-done.2
  921.2 15.6 %collective-permute-done.3 = bf16[512,768]{0,1:T(8,128)(2,1)} collective-permute-done((bf16[512,768]{0,1:T(8,128)(2,1)}, bf16[512,768]{0,1:T(8,128)(2,1)}, u32[]{:S(2)}, u32[]{:S(2)}) %collective-permute-start.3) | collective-permute-done | bytes 786464 | tf_op jit(solution)/shard_map/while/body/eval_jaxpr/ppermute | solution.py:16
  939.3 14.4 %collective-permute-done = bf16[512,768]{0,1:T(8,128)(2,1)} collective-permute-done((bf16[512,768]{0,1:T(8,128)(2,1)S(1)}, bf16[512,768]{0,1:T(8,128)(2,1)}, u32[]{:S(2)}, u32[]{:S(2)}) %collective-permute-start) | collective-permute-done | bytes 786464 | tf_op jit(solution)/shard_map/while/body/eval_jaxpr/ppermute | solution.py:16
  953.7 10.6 collective-permute-done.1
  986.1 6.4 bitcast_add_fusion.7
  992.5 9.3 collective-permute-done.2
  1003.2 15.6 %collective-permute-done.3 = bf16[512,768]{0,1:T(8,128)(2,1)} collective-permute-done((bf16[512,768]{0,1:T(8,128)(2,1)}, bf16[512,768]{0,1:T(8,128)(2,1)}, u32[]{:S(2)}, u32[]{:S(2)}) %collective-permute-start.3) | collective-permute-done | bytes 786464 | tf_op jit(solution)/shard_map/while/body/eval_jaxpr/ppermute | solution.py:16
  1021.3 14.4 %collective-permute-done = bf16[512,768]{0,1:T(8,128)(2,1)} collective-permute-done((bf16[512,768]{0,1:T(8,128)(2,1)S(1)}, bf16[512,768]{0,1:T(8,128)(2,1)}, u32[]{:S(2)}, u32[]{:S(2)}) %collective-permute-start) | collective-permute-done | bytes 786464 | tf_op jit(solution)/shard_map/while/body/eval_jaxpr/ppermute | solution.py:16
  1035.6 9.7 collective-permute-done.1
  1067.2 6.4 bitcast_add_fusion.7
  1073.6 9.3 collective-permute-done.2
  1084.3 15.6 %collective-permute-done.3 = bf16[512,768]{0,1:T(8,128)(2,1)} collective-permute-done((bf16[512,768]{0,1:T(8,128)(2,1)}, bf16[512,768]{0,1:T(8,128)(2,1)}, u32[]{:S(2)}, u32[]{:S(2)}) %collective-permute-start.3) | collective-permute-done | bytes 786464 | tf_op jit(solution)/shard_map/while/body/eval_jaxpr/ppermute | solution.py:16
  1102.3 14.4 %collective-permute-done = bf16[512,768]{0,1:T(8,128)(2,1)} collective-permute-done((bf16[512,768]{0,1:T(8,128)(2,1)S(1)}, bf16[512,768]{0,1:T(8,128)(2,1)}, u32[]{:S(2)}, u32[]{:S(2)}) %collective-permute-start) | collective-permute-done | bytes 786464 | tf_op jit(solution)/shard_map/while/body/eval_jaxpr/ppermute | solution.py:16
  1116.7 8.9 collective-permute-done.1
  1138.7 36.9 %reduce-scatter.5.cloned.1.call-done = bf16[192,2304]{1,0:T(8,128)(2,1)} async-done(((bf16[768,2304]{1,0:T(8,128)(2,1)}), bf16[192,2304]{1,0:T(8,128)(2,1)}) %reduce-scatter.5.cloned.1.call-update) | async-done | bytes 884752 | tf_op jit(solution)/shard_map/reduce_scatter | solution.py:273
  1188.4 22.0 %all-reduce.6 = (bf16[192]{0:T(256)(128)(2,1)S(1)}, bf16[192]{0:T(256)(128)(2,1)S(1)}) all-reduce(bf16[192]{0:T(256)(128)(2,1)S(1)} %dynamic-slice.3, bf16[192]{0:T(256)(128)(2,1)S(1)} %dynamic-slice.5), channel_id=1, replica_groups=mesh['ctx'=8,'dp'=4] {'ctx'}, use_global_device_ids=true, to_apply=%region_17.18 | all-reduce | flops 384 | bytes 1536 | tf_op jit(solution)/shard_map/psum | solution.py:287
  1217.0 53.4 %all-reduce.12.cloned.1.call-done = (bf16[192,768]{1,0:T(8,128)(2,1)}, bf16[192,2304]{1,0:T(8,128)(2,1)}, bf16[288,768]{1,0:T(8,128)(2,1)}) async-done(((bf16[192,768]{1,0:T(8,128)(2,1)}, bf16[192,2304]{1,0:T(8,128)(2,1)}, bf16[288,768]{1,0:T(8,128)(2,1)}), (bf16[192,768]{1,0:T(8,128)(2,1)}, bf16[192,2304]{1,0:T(8,128)(2,1)}, bf16[288,768]{1,0:T(8,128)(2,1)})) %all-reduce.12.cloned.1.call-update) | async-done | bytes 1622032 | tf_op jit(solution)/shard_map/psum | solution.py:290
  1274.8 105.2 %all-gather.21.cloned.1.call-done = bf16[1536,2304]{1,0:T(8,128)(2,1)} async-done(((bf16[192,2304]{1,0:T(8,128)(2,1)}), bf16[1536,2304]{1,0:T(8,128)(2,1)}) %all-gather.21.cloned.1.call-update) | async-done | bytes 7077904 | tf_op jit(solution)/shard_map/all_gather | solution.py:11
  (467 shorter events, 389.9 us)
Async XLA Ops:
  7.2 13.9 copy-start.14
  7.2 35.9 %all-gather.9.cloned.1.call-start = ((), (), s32[]{:S(2)}) async-start(), calls=%async_computation.4 | async-start | bytes 4423680 | tf_op jit(solution)/shard_map/all_gather | solution.py:89
  7.9 149.0 %all-gather.11.cloned.1.call-start = ((), (), s32[]{:S(2)}) async-start(), calls=%async_computation.5 | async-start | bytes 7077888 | tf_op jit(solution)/shard_map/all_gather | solution.py:132
  20.0 28.8 %copy-start.37 = (f32[768]{0:T(1024)}, f32[768]{0:T(1024)S(1)}, u32[]{:S(2)}) copy-start(f32[768]{0:T(1024)S(1)} %convert_element_type.149) | copy-start | bytes 9220
  21.0 34.9 %copy-start.23 = (f32[512,64]{0,1:T(8,128)}, f32[512,64]{0,1:T(8,128)S(1)}, u32[]{:S(2)}) copy-start(f32[512,64]{0,1:T(8,128)S(1)} %pad_maximum_fusion.4) | copy-start | bytes 393220
  21.0 32.8 %copy-start.28 = (f32[512,64]{0,1:T(8,128)}, f32[512,64]{0,1:T(8,128)S(1)}, u32[]{:S(2)}) copy-start(f32[512,64]{0,1:T(8,128)S(1)} %pad_maximum_fusion.5) | copy-start | bytes 393220
  21.2 27.6 %copy-start.39 = (f32[512]{0:T(512)}, f32[512]{0:T(512)S(1)}, u32[]{:S(2)}) copy-start(f32[512]{0:T(512)S(1)} %broadcast_multiply_fusion.3) | copy-start | bytes 6148
  21.6 27.2 %copy-start.45 = (f32[512]{0:T(512)}, f32[512]{0:T(512)S(1)}, u32[]{:S(2)}) copy-start(f32[512]{0:T(512)S(1)} %fusion.44) | copy-start | bytes 6148
  21.6 27.2 %copy-start.41 = (f32[512]{0:T(512)}, f32[512]{0:T(512)S(1)}, u32[]{:S(2)}) copy-start(f32[512]{0:T(512)S(1)} %fusion.75) | copy-start | bytes 6148
  57.3 199.4 %all-gather.13.cloned.1.call-start = ((), (), s32[]{:S(2)}) async-start(), calls=%async_computation.6 | async-start | bytes 7077888 | tf_op jit(solution)/shard_map/all_gather | solution.py:133
  59.8 355.8 %all-gather.15.cloned.1.call-start = ((), (), s32[]{:S(2)}) async-start(), calls=%async_computation.7 | async-start | bytes 1474560 | tf_op jit(solution)/shard_map/all_gather | solution.py:90
  60.4 359.2 %all-gather.17.cloned.1.call-start = ((), (), s32[]{:S(2)}) async-start(), calls=%async_computation.8 | async-start | bytes 4423680 | tf_op jit(solution)/shard_map/all_gather | solution.py:91
  61.0 365.4 %all-gather.19.cloned.1.call-start = ((), (), s32[]{:S(2)}) async-start(), calls=%async_computation.9 | async-start | bytes 2211840 | tf_op jit(solution)/shard_map/all_gather | solution.py:92
  61.5 1076.2 %reduce-scatter.7.cloned.1.call-start = ((), (), s32[]{:S(2)}) async-start(), calls=%async_computation.11 | async-start | bytes 1474560 | tf_op jit(solution)/shard_map/reduce_scatter | solution.py:276
  435.7 11.0 copy-start.30
  446.6 691.1 %reduce-scatter.11.cloned.1.call-start = ((), (), s32[]{:S(2)}) async-start(), calls=%async_computation.13 | async-start | bytes 2211840 | tf_op jit(solution)/shard_map/reduce_scatter | solution.py:282
  449.0 688.8 %reduce-scatter.9.cloned.1.call-start = ((), (), s32[]{:S(2)}) async-start(), calls=%async_computation.12 | async-start | bytes 4423680 | tf_op jit(solution)/shard_map/reduce_scatter | solution.py:279
  460.9 714.6 %reduce-scatter.5.cloned.1.call-start = ((), (), s32[]{:S(2)}) async-start(), calls=%async_computation.10 | async-start | bytes 4423680 | tf_op jit(solution)/shard_map/reduce_scatter | solution.py:273
  461.0 664.6 %copy-start.29 = (f32[512,64]{0,1:T(8,128)S(1)}, f32[512,64]{0,1:T(8,128)}, u32[]{:S(2)}) copy-start(f32[512,64]{0,1:T(8,128)} %copy-done.28) | copy-start | bytes 393220
  474.0 23.3 %collective-permute-start.2 = (bf16[512,768]{0,1:T(8,128)(2,1)}, bf16[512,768]{0,1:T(8,128)(2,1)S(1)}, u32[]{:S(2)}, u32[]{:S(2)}) collective-permute-start(bf16[512,768]{0,1:T(8,128)(2,1)} %fusion.151), channel_id=1, source_target_pairs={{0,4},{4,8},{8,12},{12,16},{16,20},{20,24},{24,28},{28,0},{1,5},{5... | collective-permute-start | bytes 2359304 | tf_op jit(solution)/shard_map/while/body/eval_jaxpr/ppermute | solution.py:16
  483.3 31.0 %collective-permute-start.3 = (bf16[512,768]{0,1:T(8,128)(2,1)}, bf16[512,768]{0,1:T(8,128)(2,1)}, u32[]{:S(2)}, u32[]{:S(2)}) collective-permute-start(bf16[512,768]{0,1:T(8,128)(2,1)} %fusion.153), channel_id=1, source_target_pairs={{0,4},{4,8},{8,12},{12,16},{16,20},{20,24},{24,28},{28,0},{1,5},{5... | collective-permute-start | bytes 2359304 | tf_op jit(solution)/shard_map/while/body/eval_jaxpr/ppermute | solution.py:16
  483.3 47.8 %collective-permute-start = (bf16[512,768]{0,1:T(8,128)(2,1)S(1)}, bf16[512,768]{0,1:T(8,128)(2,1)}, u32[]{:S(2)}, u32[]{:S(2)}) collective-permute-start(bf16[512,768]{0,1:T(8,128)(2,1)S(1)} %copy.58), channel_id=1, source_target_pairs={{0,4},{4,8},{8,12},{12,16},{16,20},{20,24},{24,28},{28,0},{1,5},{5... | collective-permute-start | bytes 2359304 | tf_op jit(solution)/shard_map/while/body/eval_jaxpr/ppermute | solution.py:16
  483.3 62.7 %collective-permute-start.1 = (bf16[512,768]{0,1:T(8,128)(2,1)S(1)}, bf16[512,768]{0,1:T(8,128)(2,1)}, u32[]{:S(2)}, u32[]{:S(2)}) collective-permute-start(bf16[512,768]{0,1:T(8,128)(2,1)S(1)} %copy-done.6), channel_id=1, source_target_pairs={{0,4},{4,8},{8,12},{12,16},{16,20},{20,24},{24,28},{28,0},{1,5},{5... | collective-permute-start | bytes 2359304 | tf_op jit(solution)/shard_map/while/body/eval_jaxpr/ppermute | solution.py:16
  498.7 47.3 %copy-start.4 = (bf16[512,12,64]{0,2,1:T(8,128)(2,1)S(1)}, bf16[512,12,64]{0,2,1:T(8,128)(2,1)}, u32[]{:S(2)}) copy-start(bf16[512,12,64]{0,2,1:T(8,128)(2,1)} %copy-done.3) | copy-start | bytes 2359300 | tf_op jit(solution)/shard_map/while
  560.2 23.3 %collective-permute-start.2 = (bf16[512,768]{0,1:T(8,128)(2,1)}, bf16[512,768]{0,1:T(8,128)(2,1)S(1)}, u32[]{:S(2)}, u32[]{:S(2)}) collective-permute-start(bf16[512,768]{0,1:T(8,128)(2,1)} %fusion.151), channel_id=1, source_target_pairs={{0,4},{4,8},{8,12},{12,16},{16,20},{20,24},{24,28},{28,0},{1,5},{5... | collective-permute-start | bytes 2359304 | tf_op jit(solution)/shard_map/while/body/eval_jaxpr/ppermute | solution.py:16
  567.8 32.7 %collective-permute-start.3 = (bf16[512,768]{0,1:T(8,128)(2,1)}, bf16[512,768]{0,1:T(8,128)(2,1)}, u32[]{:S(2)}, u32[]{:S(2)}) collective-permute-start(bf16[512,768]{0,1:T(8,128)(2,1)} %fusion.153), channel_id=1, source_target_pairs={{0,4},{4,8},{8,12},{12,16},{16,20},{20,24},{24,28},{28,0},{1,5},{5... | collective-permute-start | bytes 2359304 | tf_op jit(solution)/shard_map/while/body/eval_jaxpr/ppermute | solution.py:16
  568.8 48.6 %collective-permute-start = (bf16[512,768]{0,1:T(8,128)(2,1)S(1)}, bf16[512,768]{0,1:T(8,128)(2,1)}, u32[]{:S(2)}, u32[]{:S(2)}) collective-permute-start(bf16[512,768]{0,1:T(8,128)(2,1)S(1)} %copy.58), channel_id=1, source_target_pairs={{0,4},{4,8},{8,12},{12,16},{16,20},{20,24},{24,28},{28,0},{1,5},{5... | collective-permute-start | bytes 2359304 | tf_op jit(solution)/shard_map/while/body/eval_jaxpr/ppermute | solution.py:16
  568.9 62.5 %collective-permute-start.1 = (bf16[512,768]{0,1:T(8,128)(2,1)S(1)}, bf16[512,768]{0,1:T(8,128)(2,1)}, u32[]{:S(2)}, u32[]{:S(2)}) collective-permute-start(bf16[512,768]{0,1:T(8,128)(2,1)S(1)} %copy-done.6), channel_id=1, source_target_pairs={{0,4},{4,8},{8,12},{12,16},{16,20},{20,24},{24,28},{28,0},{1,5},{5... | collective-permute-start | bytes 2359304 | tf_op jit(solution)/shard_map/while/body/eval_jaxpr/ppermute | solution.py:16
  584.9 46.5 %copy-start.4 = (bf16[512,12,64]{0,2,1:T(8,128)(2,1)S(1)}, bf16[512,12,64]{0,2,1:T(8,128)(2,1)}, u32[]{:S(2)}) copy-start(bf16[512,12,64]{0,2,1:T(8,128)(2,1)} %copy-done.3) | copy-start | bytes 2359300 | tf_op jit(solution)/shard_map/while
  645.6 23.3 %collective-permute-start.2 = (bf16[512,768]{0,1:T(8,128)(2,1)}, bf16[512,768]{0,1:T(8,128)(2,1)S(1)}, u32[]{:S(2)}, u32[]{:S(2)}) collective-permute-start(bf16[512,768]{0,1:T(8,128)(2,1)} %fusion.151), channel_id=1, source_target_pairs={{0,4},{4,8},{8,12},{12,16},{16,20},{20,24},{24,28},{28,0},{1,5},{5... | collective-permute-start | bytes 2359304 | tf_op jit(solution)/shard_map/while/body/eval_jaxpr/ppermute | solution.py:16
  653.1 32.7 %collective-permute-start.3 = (bf16[512,768]{0,1:T(8,128)(2,1)}, bf16[512,768]{0,1:T(8,128)(2,1)}, u32[]{:S(2)}, u32[]{:S(2)}) collective-permute-start(bf16[512,768]{0,1:T(8,128)(2,1)} %fusion.153), channel_id=1, source_target_pairs={{0,4},{4,8},{8,12},{12,16},{16,20},{20,24},{24,28},{28,0},{1,5},{5... | collective-permute-start | bytes 2359304 | tf_op jit(solution)/shard_map/while/body/eval_jaxpr/ppermute | solution.py:16
  653.7 49.0 %collective-permute-start = (bf16[512,768]{0,1:T(8,128)(2,1)S(1)}, bf16[512,768]{0,1:T(8,128)(2,1)}, u32[]{:S(2)}, u32[]{:S(2)}) collective-permute-start(bf16[512,768]{0,1:T(8,128)(2,1)S(1)} %copy.58), channel_id=1, source_target_pairs={{0,4},{4,8},{8,12},{12,16},{16,20},{20,24},{24,28},{28,0},{1,5},{5... | collective-permute-start | bytes 2359304 | tf_op jit(solution)/shard_map/while/body/eval_jaxpr/ppermute | solution.py:16
  653.8 62.1 %collective-permute-start.1 = (bf16[512,768]{0,1:T(8,128)(2,1)S(1)}, bf16[512,768]{0,1:T(8,128)(2,1)}, u32[]{:S(2)}, u32[]{:S(2)}) collective-permute-start(bf16[512,768]{0,1:T(8,128)(2,1)S(1)} %copy-done.6), channel_id=1, source_target_pairs={{0,4},{4,8},{8,12},{12,16},{16,20},{20,24},{24,28},{28,0},{1,5},{5... | collective-permute-start | bytes 2359304 | tf_op jit(solution)/shard_map/while/body/eval_jaxpr/ppermute | solution.py:16
  670.3 45.6 %copy-start.4 = (bf16[512,12,64]{0,2,1:T(8,128)(2,1)S(1)}, bf16[512,12,64]{0,2,1:T(8,128)(2,1)}, u32[]{:S(2)}) copy-start(bf16[512,12,64]{0,2,1:T(8,128)(2,1)} %copy-done.3) | copy-start | bytes 2359300 | tf_op jit(solution)/shard_map/while
  730.1 23.3 %collective-permute-start.2 = (bf16[512,768]{0,1:T(8,128)(2,1)}, bf16[512,768]{0,1:T(8,128)(2,1)S(1)}, u32[]{:S(2)}, u32[]{:S(2)}) collective-permute-start(bf16[512,768]{0,1:T(8,128)(2,1)} %fusion.151), channel_id=1, source_target_pairs={{0,4},{4,8},{8,12},{12,16},{16,20},{20,24},{24,28},{28,0},{1,5},{5... | collective-permute-start | bytes 2359304 | tf_op jit(solution)/shard_map/while/body/eval_jaxpr/ppermute | solution.py:16
  737.7 32.7 %collective-permute-start.3 = (bf16[512,768]{0,1:T(8,128)(2,1)}, bf16[512,768]{0,1:T(8,128)(2,1)}, u32[]{:S(2)}, u32[]{:S(2)}) collective-permute-start(bf16[512,768]{0,1:T(8,128)(2,1)} %fusion.153), channel_id=1, source_target_pairs={{0,4},{4,8},{8,12},{12,16},{16,20},{20,24},{24,28},{28,0},{1,5},{5... | collective-permute-start | bytes 2359304 | tf_op jit(solution)/shard_map/while/body/eval_jaxpr/ppermute | solution.py:16
  737.7 49.5 %collective-permute-start = (bf16[512,768]{0,1:T(8,128)(2,1)S(1)}, bf16[512,768]{0,1:T(8,128)(2,1)}, u32[]{:S(2)}, u32[]{:S(2)}) collective-permute-start(bf16[512,768]{0,1:T(8,128)(2,1)S(1)} %copy.58), channel_id=1, source_target_pairs={{0,4},{4,8},{8,12},{12,16},{16,20},{20,24},{24,28},{28,0},{1,5},{5... | collective-permute-start | bytes 2359304 | tf_op jit(solution)/shard_map/while/body/eval_jaxpr/ppermute | solution.py:16
  737.8 61.7 %collective-permute-start.1 = (bf16[512,768]{0,1:T(8,128)(2,1)S(1)}, bf16[512,768]{0,1:T(8,128)(2,1)}, u32[]{:S(2)}, u32[]{:S(2)}) collective-permute-start(bf16[512,768]{0,1:T(8,128)(2,1)S(1)} %copy-done.6), channel_id=1, source_target_pairs={{0,4},{4,8},{8,12},{12,16},{16,20},{20,24},{24,28},{28,0},{1,5},{5... | collective-permute-start | bytes 2359304 | tf_op jit(solution)/shard_map/while/body/eval_jaxpr/ppermute | solution.py:16
  754.8 44.7 %copy-start.4 = (bf16[512,12,64]{0,2,1:T(8,128)(2,1)S(1)}, bf16[512,12,64]{0,2,1:T(8,128)(2,1)}, u32[]{:S(2)}) copy-start(bf16[512,12,64]{0,2,1:T(8,128)(2,1)} %copy-done.3) | copy-start | bytes 2359300 | tf_op jit(solution)/shard_map/while
  813.8 23.3 %collective-permute-start.2 = (bf16[512,768]{0,1:T(8,128)(2,1)}, bf16[512,768]{0,1:T(8,128)(2,1)S(1)}, u32[]{:S(2)}, u32[]{:S(2)}) collective-permute-start(bf16[512,768]{0,1:T(8,128)(2,1)} %fusion.151), channel_id=1, source_target_pairs={{0,4},{4,8},{8,12},{12,16},{16,20},{20,24},{24,28},{28,0},{1,5},{5... | collective-permute-start | bytes 2359304 | tf_op jit(solution)/shard_map/while/body/eval_jaxpr/ppermute | solution.py:16
  821.3 32.7 %collective-permute-start.3 = (bf16[512,768]{0,1:T(8,128)(2,1)}, bf16[512,768]{0,1:T(8,128)(2,1)}, u32[]{:S(2)}, u32[]{:S(2)}) collective-permute-start(bf16[512,768]{0,1:T(8,128)(2,1)} %fusion.153), channel_id=1, source_target_pairs={{0,4},{4,8},{8,12},{12,16},{16,20},{20,24},{24,28},{28,0},{1,5},{5... | collective-permute-start | bytes 2359304 | tf_op jit(solution)/shard_map/while/body/eval_jaxpr/ppermute | solution.py:16
  821.3 49.6 %collective-permute-start = (bf16[512,768]{0,1:T(8,128)(2,1)S(1)}, bf16[512,768]{0,1:T(8,128)(2,1)}, u32[]{:S(2)}, u32[]{:S(2)}) collective-permute-start(bf16[512,768]{0,1:T(8,128)(2,1)S(1)} %copy.58), channel_id=1, source_target_pairs={{0,4},{4,8},{8,12},{12,16},{16,20},{20,24},{24,28},{28,0},{1,5},{5... | collective-permute-start | bytes 2359304 | tf_op jit(solution)/shard_map/while/body/eval_jaxpr/ppermute | solution.py:16
  821.3 61.0 %collective-permute-start.1 = (bf16[512,768]{0,1:T(8,128)(2,1)S(1)}, bf16[512,768]{0,1:T(8,128)(2,1)}, u32[]{:S(2)}, u32[]{:S(2)}) collective-permute-start(bf16[512,768]{0,1:T(8,128)(2,1)S(1)} %copy-done.6), channel_id=1, source_target_pairs={{0,4},{4,8},{8,12},{12,16},{16,20},{20,24},{24,28},{28,0},{1,5},{5... | collective-permute-start | bytes 2359304 | tf_op jit(solution)/shard_map/while/body/eval_jaxpr/ppermute | solution.py:16
  838.4 43.9 %copy-start.4 = (bf16[512,12,64]{0,2,1:T(8,128)(2,1)S(1)}, bf16[512,12,64]{0,2,1:T(8,128)(2,1)}, u32[]{:S(2)}) copy-start(bf16[512,12,64]{0,2,1:T(8,128)(2,1)} %copy-done.3) | copy-start | bytes 2359300 | tf_op jit(solution)/shard_map/while
  896.6 23.3 %collective-permute-start.2 = (bf16[512,768]{0,1:T(8,128)(2,1)}, bf16[512,768]{0,1:T(8,128)(2,1)S(1)}, u32[]{:S(2)}, u32[]{:S(2)}) collective-permute-start(bf16[512,768]{0,1:T(8,128)(2,1)} %fusion.151), channel_id=1, source_target_pairs={{0,4},{4,8},{8,12},{12,16},{16,20},{20,24},{24,28},{28,0},{1,5},{5... | collective-permute-start | bytes 2359304 | tf_op jit(solution)/shard_map/while/body/eval_jaxpr/ppermute | solution.py:16
  904.1 32.7 %collective-permute-start.3 = (bf16[512,768]{0,1:T(8,128)(2,1)}, bf16[512,768]{0,1:T(8,128)(2,1)}, u32[]{:S(2)}, u32[]{:S(2)}) collective-permute-start(bf16[512,768]{0,1:T(8,128)(2,1)} %fusion.153), channel_id=1, source_target_pairs={{0,4},{4,8},{8,12},{12,16},{16,20},{20,24},{24,28},{28,0},{1,5},{5... | collective-permute-start | bytes 2359304 | tf_op jit(solution)/shard_map/while/body/eval_jaxpr/ppermute | solution.py:16
  904.1 49.6 %collective-permute-start = (bf16[512,768]{0,1:T(8,128)(2,1)S(1)}, bf16[512,768]{0,1:T(8,128)(2,1)}, u32[]{:S(2)}, u32[]{:S(2)}) collective-permute-start(bf16[512,768]{0,1:T(8,128)(2,1)S(1)} %copy.58), channel_id=1, source_target_pairs={{0,4},{4,8},{8,12},{12,16},{16,20},{20,24},{24,28},{28,0},{1,5},{5... | collective-permute-start | bytes 2359304 | tf_op jit(solution)/shard_map/while/body/eval_jaxpr/ppermute | solution.py:16
  904.1 60.1 %collective-permute-start.1 = (bf16[512,768]{0,1:T(8,128)(2,1)S(1)}, bf16[512,768]{0,1:T(8,128)(2,1)}, u32[]{:S(2)}, u32[]{:S(2)}) collective-permute-start(bf16[512,768]{0,1:T(8,128)(2,1)S(1)} %copy-done.6), channel_id=1, source_target_pairs={{0,4},{4,8},{8,12},{12,16},{16,20},{20,24},{24,28},{28,0},{1,5},{5... | collective-permute-start | bytes 2359304 | tf_op jit(solution)/shard_map/while/body/eval_jaxpr/ppermute | solution.py:16
  921.2 43.0 %copy-start.4 = (bf16[512,12,64]{0,2,1:T(8,128)(2,1)S(1)}, bf16[512,12,64]{0,2,1:T(8,128)(2,1)}, u32[]{:S(2)}) copy-start(bf16[512,12,64]{0,2,1:T(8,128)(2,1)} %copy-done.3) | copy-start | bytes 2359300 | tf_op jit(solution)/shard_map/while
  978.5 23.3 %collective-permute-start.2 = (bf16[512,768]{0,1:T(8,128)(2,1)}, bf16[512,768]{0,1:T(8,128)(2,1)S(1)}, u32[]{:S(2)}, u32[]{:S(2)}) collective-permute-start(bf16[512,768]{0,1:T(8,128)(2,1)} %fusion.151), channel_id=1, source_target_pairs={{0,4},{4,8},{8,12},{12,16},{16,20},{20,24},{24,28},{28,0},{1,5},{5... | collective-permute-start | bytes 2359304 | tf_op jit(solution)/shard_map/while/body/eval_jaxpr/ppermute | solution.py:16
  986.0 32.7 %collective-permute-start.3 = (bf16[512,768]{0,1:T(8,128)(2,1)}, bf16[512,768]{0,1:T(8,128)(2,1)}, u32[]{:S(2)}, u32[]{:S(2)}) collective-permute-start(bf16[512,768]{0,1:T(8,128)(2,1)} %fusion.153), channel_id=1, source_target_pairs={{0,4},{4,8},{8,12},{12,16},{16,20},{20,24},{24,28},{28,0},{1,5},{5... | collective-permute-start | bytes 2359304 | tf_op jit(solution)/shard_map/while/body/eval_jaxpr/ppermute | solution.py:16
  986.0 49.6 %collective-permute-start = (bf16[512,768]{0,1:T(8,128)(2,1)S(1)}, bf16[512,768]{0,1:T(8,128)(2,1)}, u32[]{:S(2)}, u32[]{:S(2)}) collective-permute-start(bf16[512,768]{0,1:T(8,128)(2,1)S(1)} %copy.58), channel_id=1, source_target_pairs={{0,4},{4,8},{8,12},{12,16},{16,20},{20,24},{24,28},{28,0},{1,5},{5... | collective-permute-start | bytes 2359304 | tf_op jit(solution)/shard_map/while/body/eval_jaxpr/ppermute | solution.py:16
  986.1 59.3 %collective-permute-start.1 = (bf16[512,768]{0,1:T(8,128)(2,1)S(1)}, bf16[512,768]{0,1:T(8,128)(2,1)}, u32[]{:S(2)}, u32[]{:S(2)}) collective-permute-start(bf16[512,768]{0,1:T(8,128)(2,1)S(1)} %copy-done.6), channel_id=1, source_target_pairs={{0,4},{4,8},{8,12},{12,16},{16,20},{20,24},{24,28},{28,0},{1,5},{5... | collective-permute-start | bytes 2359304 | tf_op jit(solution)/shard_map/while/body/eval_jaxpr/ppermute | solution.py:16
  1003.2 42.2 %copy-start.4 = (bf16[512,12,64]{0,2,1:T(8,128)(2,1)S(1)}, bf16[512,12,64]{0,2,1:T(8,128)(2,1)}, u32[]{:S(2)}) copy-start(bf16[512,12,64]{0,2,1:T(8,128)(2,1)} %copy-done.3) | copy-start | bytes 2359300 | tf_op jit(solution)/shard_map/while
  1059.6 23.3 %collective-permute-start.2 = (bf16[512,768]{0,1:T(8,128)(2,1)}, bf16[512,768]{0,1:T(8,128)(2,1)S(1)}, u32[]{:S(2)}, u32[]{:S(2)}) collective-permute-start(bf16[512,768]{0,1:T(8,128)(2,1)} %fusion.151), channel_id=1, source_target_pairs={{0,4},{4,8},{8,12},{12,16},{16,20},{20,24},{24,28},{28,0},{1,5},{5... | collective-permute-start | bytes 2359304 | tf_op jit(solution)/shard_map/while/body/eval_jaxpr/ppermute | solution.py:16
  1067.1 32.7 %collective-permute-start.3 = (bf16[512,768]{0,1:T(8,128)(2,1)}, bf16[512,768]{0,1:T(8,128)(2,1)}, u32[]{:S(2)}, u32[]{:S(2)}) collective-permute-start(bf16[512,768]{0,1:T(8,128)(2,1)} %fusion.153), channel_id=1, source_target_pairs={{0,4},{4,8},{8,12},{12,16},{16,20},{20,24},{24,28},{28,0},{1,5},{5... | collective-permute-start | bytes 2359304 | tf_op jit(solution)/shard_map/while/body/eval_jaxpr/ppermute | solution.py:16
  1067.1 49.6 %collective-permute-start = (bf16[512,768]{0,1:T(8,128)(2,1)S(1)}, bf16[512,768]{0,1:T(8,128)(2,1)}, u32[]{:S(2)}, u32[]{:S(2)}) collective-permute-start(bf16[512,768]{0,1:T(8,128)(2,1)S(1)} %copy.58), channel_id=1, source_target_pairs={{0,4},{4,8},{8,12},{12,16},{16,20},{20,24},{24,28},{28,0},{1,5},{5... | collective-permute-start | bytes 2359304 | tf_op jit(solution)/shard_map/while/body/eval_jaxpr/ppermute | solution.py:16
  1067.1 58.4 %collective-permute-start.1 = (bf16[512,768]{0,1:T(8,128)(2,1)S(1)}, bf16[512,768]{0,1:T(8,128)(2,1)}, u32[]{:S(2)}, u32[]{:S(2)}) collective-permute-start(bf16[512,768]{0,1:T(8,128)(2,1)S(1)} %copy-done.6), channel_id=1, source_target_pairs={{0,4},{4,8},{8,12},{12,16},{16,20},{20,24},{24,28},{28,0},{1,5},{5... | collective-permute-start | bytes 2359304 | tf_op jit(solution)/shard_map/while/body/eval_jaxpr/ppermute | solution.py:16
  1084.3 41.3 %copy-start.4 = (bf16[512,12,64]{0,2,1:T(8,128)(2,1)S(1)}, bf16[512,12,64]{0,2,1:T(8,128)(2,1)}, u32[]{:S(2)}) copy-start(bf16[512,12,64]{0,2,1:T(8,128)(2,1)} %copy-done.3) | copy-start | bytes 2359300 | tf_op jit(solution)/shard_map/while
  1137.7 132.7 %all-reduce.12.cloned.1.call-start = ((), (), s32[]{:S(2)}) async-start(), calls=%async_computation.15 | async-start | bytes 3244032 | tf_op jit(solution)/shard_map/psum | solution.py:290
  1138.4 241.6 %all-gather.21.cloned.1.call-start = ((), (), s32[]{:S(2)}) async-start(), calls=%async_computation.14 | async-start | bytes 7962624 | tf_op jit(solution)/shard_map/all_gather | solution.py:11
  1180.5 31.0 %copy-start.13 = (f32[512,768]{1,0:T(8,128)S(1)}, f32[512,768]{1,0:T(8,128)}, u32[]{:S(2)}) copy-start(f32[512,768]{1,0:T(8,128)} %copy-done.12) | copy-start | bytes 4718596
  1180.5 31.0 %copy-start.26 = (bf16[1,512,768]{2,1,0:T(8,128)(2,1)S(1)}, bf16[1,512,768]{2,1,0:T(8,128)(2,1)}, u32[]{:S(2)}) copy-start(bf16[1,512,768]{2,1,0:T(8,128)(2,1)} %param.14) | copy-start | bytes 2359300
  1180.5 31.0 %copy-start.44 = (f32[512]{0:T(512)S(1)}, f32[512]{0:T(512)}, u32[]{:S(2)}) copy-start(f32[512]{0:T(512)} %copy-done.43) | copy-start | bytes 6148
  (87 other events, 320.0 us)
Sparse Core Ops, SparseCore 0:
  9.5 33.4 all-gather.8
  57.4 99.4 all-gather.10
  158.9 97.6 all-gather.12
  258.0 15.6 all-gather.14
  275.1 30.7 all-gather.16
  307.3 20.7 all-gather.18
  446.7 23.7 reduce-scatter.6
  473.7 29.1 reduce-scatter.10
  505.5 40.3 reduce-scatter.8
  1137.8 37.6 reduce-scatter.4
  1179.4 90.9 all-reduce.11
  1272.4 107.5 all-gather.20
